TPU v7x, 512 devices: a whole 4x4x16 slice. The times are simulated.
512 devices in a mesh: dp: 32 (over z, core), ctx: 16 (over y, x).
Axes of the slice: x: 4, y: 4, z: 16, core: 2. Of those that a mesh axis runs over, the one named last changes fastest.
Arguments:
- queries: bfloat16 [65536, 4096], P(('dp', 'ctx')), parts along dimension 0, may hold values from -9 to 9
- keys: bfloat16 [65536, 512], P(('dp', 'ctx')), parts along dimension 0, may hold values from -9 to 9
- values: bfloat16 [65536, 512], P(('dp', 'ctx')), parts along dimension 0, may hold values from -6 to 6
- grad_out: bfloat16 [65536, 4096], P(('dp', 'ctx')), parts along dimension 0, may hold values from -6 to 6
- doc_blocks: int32 [256], P('dp'), parts along dimension 0, may hold values from 1 to 9, 32 in all
Outputs:
- output: bfloat16 [65536, 4096], P(('dp', 'ctx')), parts along dimension 0
- query_grad: bfloat16 [65536, 4096], P(('dp', 'ctx')), parts along dimension 0
- key_grad: bfloat16 [65536, 512], P(('dp', 'ctx')), parts along dimension 0
- value_grad: bfloat16 [65536, 512], P(('dp', 'ctx')), parts along dimension 0
There are 32 independent parts, one for each index of `dp`. A program takes and returns all parts, laid end to end along the dimension named above; each array names one. Nothing has to cross between parts.
Inputs may be any that keep to these rules, and one draw needn't show every extreme that they name: doc_blocks sums to 32; the longest document has exactly 9 blocks.
All inputs are finite; a program needn't handle non-finite values.
Results may differ from a plain program's by a relative error of at most 0.012.
The roundings to bfloat16 on the way count: a program that leaves them out, or rounds other values in their place, can miss the bound.
Values may be sent and summed in bfloat16 or wider, within the bound.
A program may use at most 128 MiB of HBM per device.

v0:
```python
import jax
import jax.numpy as jnp
from jax import lax
from jax.sharding import PartitionSpec as P

HEADS = 32
KV_HEADS = 4
HEAD_DIM = 128


def shifted(x, axis, by):
    length = lax.axis_size(axis)
    pairs = [(i, i + by) for i in range(length) if 0 <= i + by < length]
    return lax.ppermute(x, axis, pairs)


def as_sent(x):

    def short(part):
        return part.astype(jnp.bfloat16) if part.dtype == jnp.float32 else part

    return jax.tree.map(short, x)


def split_pair(kv_block, kv_width):
    rows_count = kv_block.shape[0]
    key_part = kv_block[:, :kv_width].reshape(rows_count, KV_HEADS, HEAD_DIM)
    value_part = kv_block[:, kv_width:].reshape(rows_count, KV_HEADS, HEAD_DIM)
    return (key_part, value_part)


def masked_scores(query_rows, key_part, on_diagonal, lower_tri, score_scale):
    scores = (
        jnp.einsum("igqe,jge->gqij", query_rows, key_part, preferred_element_type=jnp.float32)
        * score_scale
    )
    allowed = jnp.where(on_diagonal, lower_tri, True)
    return jnp.where(allowed, scores, -jnp.inf)


def local(queries, keys, values, grad_out, doc_blocks):
    members = lax.axis_size("ctx")
    device = lax.axis_index("ctx")
    rows_dev = queries.shape[0]
    half_rows = rows_dev // 2
    groups = HEADS // KV_HEADS
    kv_width = KV_HEADS * HEAD_DIM
    score_scale = HEAD_DIM ** (-0.5)
    doc_reach = max(members // 2 + 1, 4) - 1
    last_block = 2 * members - 1
    doc_ends = jnp.cumsum(doc_blocks)
    own_index = jnp.stack([device, last_block - device])
    query_own = queries.reshape(2, half_rows, KV_HEADS, groups, HEAD_DIM)
    grad_own = grad_out.reshape(2, half_rows, KV_HEADS, groups, HEAD_DIM)
    pair_own = jnp.concatenate([keys, values], axis=1).reshape(2, half_rows, 2 * kv_width)
    blocks = [pair_own[0], pair_own[1]]
    indices = [own_index[0], own_index[1]]
    for offset in range(1, doc_reach + 1):
        from_below = shifted(pair_own[0], "ctx", offset)
        blocks.append(from_below)
        indices.append(jnp.where(device - offset >= 0, device - offset, -1))
    for offset in range(1, doc_reach + 1):
        from_above = shifted(pair_own, "ctx", -offset)
        inside = device + offset < members
        blocks.append(from_above[0])
        blocks.append(from_above[1])
        indices.append(jnp.where(inside, device + offset, -1))
        indices.append(jnp.where(inside, last_block - device - offset, -1))
    cand_blocks = jnp.stack(blocks)
    cand_index = jnp.stack(indices)
    per_turn = 1
    block_doc = jnp.sum((doc_ends[None, :] <= cand_index[:, None]).astype(jnp.int32), axis=1)
    own_doc = jnp.sum((doc_ends[None, :] <= own_index[:, None]).astype(jnp.int32), axis=1)
    visible = (
        (cand_index[None, :] >= 0)
        & (cand_index[None, :] <= own_index[:, None])
        & (block_doc[None, :] == own_doc[:, None])
    )
    on_diag = cand_index[None, :] == own_index[:, None]
    cand_count = cand_blocks.shape[0]
    turn_count = cand_count // per_turn
    lower_tri = jnp.arange(half_rows)[:, None] >= jnp.arange(half_rows)[None, :]
    stacked = (
        cand_blocks.reshape(turn_count, per_turn, half_rows, 2 * kv_width),
        visible.T.reshape(turn_count, per_turn, 2),
        on_diag.T.reshape(turn_count, per_turn, 2),
    )

    def grow_stats(running, kv_block, on_diagonal, query_rows):
        run_max, run_sum = running
        key_part, value_part = split_pair(kv_block, kv_width)
        scores = masked_scores(query_rows, key_part, on_diagonal, lower_tri, score_scale)
        new_max = jnp.maximum(run_max, jnp.max(scores, axis=-1))
        new_sum = run_sum * jnp.exp(run_max - new_max) + jnp.sum(
            jnp.exp(scores - new_max[..., None]), axis=-1
        )
        return (new_max, new_sum)

    def keep_state(running, kv_block, on_diagonal, query_rows):
        return running

    def stats_turn(carried, inputs):
        kv_turn, vis_turn, diag_turn = inputs
        states = list(carried)
        for own_slot in range(2):
            states[own_slot] = lax.cond(
                vis_turn[0, own_slot],
                grow_stats,
                keep_state,
                states[own_slot],
                kv_turn[0],
                diag_turn[0, own_slot],
                query_own[own_slot],
            )
        return (tuple(states), None)

    start_stats = tuple(
        (
            (
                jnp.full((KV_HEADS, groups, half_rows), -jnp.inf, jnp.float32),
                jnp.zeros((KV_HEADS, groups, half_rows), jnp.float32),
            )
            for own_slot in range(2)
        )
    )
    final_stats = lax.scan(stats_turn, start_stats, stacked)[0]
    log_total = [
        final_stats[own_slot][0] + jnp.log(final_stats[own_slot][1]) for own_slot in range(2)
    ]

    def emit_rows(accumulated, kv_block, on_diagonal, query_rows, log_rows):
        key_part, value_part = split_pair(kv_block, kv_width)
        scores = masked_scores(query_rows, key_part, on_diagonal, lower_tri, score_scale)
        probs_low = jnp.exp(scores - log_rows[..., None]).astype(jnp.bfloat16)
        return accumulated + jnp.einsum(
            "gqij,jge->igqe", probs_low, value_part, preferred_element_type=jnp.float32
        )

    def keep_accum(accumulated, kv_block, on_diagonal, query_rows, log_rows):
        return accumulated

    def out_turn(carried, inputs):
        kv_turn, vis_turn, diag_turn = inputs
        states = list(carried)
        for own_slot in range(2):
            states[own_slot] = lax.cond(
                vis_turn[0, own_slot],
                emit_rows,
                keep_accum,
                states[own_slot],
                kv_turn[0],
                diag_turn[0, own_slot],
                query_own[own_slot],
                log_total[own_slot],
            )
        return (tuple(states), None)

    start_out = tuple(
        (jnp.zeros((half_rows, KV_HEADS, groups, HEAD_DIM), jnp.float32) for own_slot in range(2))
    )
    final_out = lax.scan(out_turn, start_out, stacked)[0]
    output_low = jnp.stack(final_out).astype(jnp.bfloat16)
    inner_rows = jnp.einsum(
        "cigqe,cigqe->cgqi", grad_own, output_low, preferred_element_type=jnp.float32
    )

    def backward(running, kv_block, on_diagonal, query_rows, grad_rows, log_rows, inner_one):
        query_grad, key_grad, value_grad = running
        key_part, value_part = split_pair(kv_block, kv_width)
        scores = masked_scores(query_rows, key_part, on_diagonal, lower_tri, score_scale)
        probs_full = jnp.exp(scores - log_rows[..., None])
        probs_low = probs_full.astype(jnp.bfloat16)
        value_grad = value_grad + jnp.einsum(
            "gqij,igqe->jge", probs_low, grad_rows, preferred_element_type=jnp.float32
        )
        prob_grad = jnp.einsum(
            "igqe,jge->gqij", grad_rows, value_part, preferred_element_type=jnp.float32
        )
        score_low = (probs_full * (prob_grad - inner_one[..., None])).astype(jnp.bfloat16)
        query_grad = query_grad + score_scale * jnp.einsum(
            "gqij,jge->igqe", score_low, key_part, preferred_element_type=jnp.float32
        )
        key_grad = key_grad + score_scale * jnp.einsum(
            "gqij,igqe->jge", score_low, query_rows, preferred_element_type=jnp.float32
        )
        return (query_grad, key_grad, value_grad)

    def keep_grads(running, kv_block, on_diagonal, query_rows, grad_rows, log_rows, inner_one):
        return running

    def grad_turn(carried, inputs):
        kv_turn, vis_turn, diag_turn = inputs
        query_grads = list(carried)
        key_grad = jnp.zeros((half_rows, KV_HEADS, HEAD_DIM), jnp.float32)
        value_grad = jnp.zeros((half_rows, KV_HEADS, HEAD_DIM), jnp.float32)
        for own_slot in range(2):
            query_grads[own_slot], key_grad, value_grad = lax.cond(
                vis_turn[0, own_slot],
                backward,
                keep_grads,
                (query_grads[own_slot], key_grad, value_grad),
                kv_turn[0],
                diag_turn[0, own_slot],
                query_own[own_slot],
                grad_own[own_slot],
                log_total[own_slot],
                inner_rows[own_slot],
            )
        pieces = [
            jnp.concatenate(
                [key_grad.reshape(half_rows, kv_width), value_grad.reshape(half_rows, kv_width)],
                axis=1,
            )
        ]
        return (tuple(query_grads), jnp.stack(pieces))

    start_grads = tuple(
        (jnp.zeros((half_rows, KV_HEADS, groups, HEAD_DIM), jnp.float32) for own_slot in range(2))
    )
    query_grads, partials = lax.scan(grad_turn, start_grads, stacked)
    partials = partials.reshape(cand_count, half_rows, 2 * kv_width)
    own_pair = partials[0:2]
    for offset in range(1, doc_reach + 1):
        back_low = shifted(as_sent(partials[1 + offset]), "ctx", -offset)
        own_pair = own_pair.at[0].add(back_low)
    for offset in range(1, doc_reach + 1):
        first_slot = 2 + doc_reach + 2 * (offset - 1)
        own_pair = own_pair + shifted(as_sent(partials[first_slot : first_slot + 2]), "ctx", offset)
    output = output_low.reshape(rows_dev, HEADS * HEAD_DIM)
    query_grad = jnp.stack(query_grads).astype(jnp.bfloat16).reshape(rows_dev, HEADS * HEAD_DIM)
    key_grad = own_pair[:, :, :kv_width].astype(jnp.bfloat16).reshape(rows_dev, kv_width)
    value_grad = own_pair[:, :, kv_width:].astype(jnp.bfloat16).reshape(rows_dev, kv_width)
    return (output, query_grad, key_grad, value_grad)


def solution(mesh):
    in_specs = (
        P(("dp", "ctx"), None),
        P(("dp", "ctx"), None),
        P(("dp", "ctx"), None),
        P(("dp", "ctx"), None),
        P("dp"),
    )
    out_specs = (
        P(("dp", "ctx"), None),
        P(("dp", "ctx"), None),
        P(("dp", "ctx"), None),
        P(("dp", "ctx"), None),
    )
    return jax.shard_map(local, mesh=mesh, in_specs=in_specs, out_specs=out_specs, check_vma=False)
```

profile of v0, /device:TPU:464, one launch (start us, length us, event | category | flops | bytes accessed | tf_op | source)
XLA Modules:
  0.0 703.0 jit_solution(6994755542368376165)
XLA Ops:
  2.6 5.4 collective-permute-start.6
  8.0 1.9 collective-permute-start.5
  9.9 1.9 collective-permute-start.4
  11.8 1.9 collective-permute-start.3
  13.8 2.1 collective-permute-start
  17.9 1.4 copy.174
  22.4 2.2 collective-permute-done
  24.6 1.9 collective-permute-start.1
  26.5 7.3 %collective-permute-done.1 = bf16[64,1024]{1,0:T(8,128)(2,1)S(1)} collective-permute-done((bf16[64,1024]{1,0:T(8,128)(2,1)S(1)}, bf16[64,1024]{1,0:T(8,128)(2,1)S(1)}, u32[]{:S(2)}, u32[]{:S(2)}) %collective-permute-start.1) | collective-permute-done | bytes 131104 | tf_op jit(solution)/shard_map/ppermute | solution.py:14
  33.9 1.9 collective-permute-start.2
  35.8 5.8 collective-permute-done.2
  42.9 6.1 collective-permute-start.15
  49.0 1.9 collective-permute-start.14
  51.0 1.9 collective-permute-start.10
  53.0 3.9 collective-permute-start.8
  56.9 1.9 collective-permute-start.9
  58.9 9.5 %collective-permute-done.8 = bf16[2,64,1024]{2,1,0:T(8,128)(2,1)S(1)} collective-permute-done((bf16[2,64,1024]{2,1,0:T(8,128)(2,1)S(1)}, bf16[2,64,1024]{2,1,0:T(8,128)(2,1)S(1)}, u32[]{:S(2)}, u32[]{:S(2)}) %collective-permute-start.8) | collective-permute-done | bytes 262176 | tf_op jit(solution)/shard_map/ppermute | solution.py:14
  68.4 1.9 collective-permute-start.11
  70.3 2.8 collective-permute-start.12
  73.2 1.9 collective-permute-start.13
  75.1 5.5 collective-permute-done.11
  80.6 2.7 collective-permute-done.12
  83.4 1.7 collective-permute-done.13
  85.2 1.8 copy-done.10
  87.0 95.5 %while.65 = (s32[]{:T(128)}, f32[4,8,64]{2,1,0:T(8,128)S(1)}, f32[4,8,64]{2,1,0:T(8,128)S(1)}, f32[4,8,64]{2,1,0:T(8,128)S(1)}, f32[4,8,64]{2,1,0:T(8,128)S(1)},...) while((s32[]{:T(128)}, f32[4,8,64]{2,1,0:T(8,128)S(1)}, ...), condition=%wide.region_12.13_spmd.clone.clone, body=%wide.region_3.12_spmd.clone.clone.sunk | while | flops 68440064 | bytes 4313407 | solution.py:126
  95.0 2.2 conditional.25
  184.3 98.5 %while.66 = (s32[]{:T(128)}, f32[64,4,8,128]{3,0,2,1:T(8,128)}, f32[64,4,8,128]{3,0,2,1:T(8,128)S(1)}, pred[26,1,2]{2,1,0:T(4,128)(4,1)}, bf16[26,1,64,1024]{3,2...) while((s32[]{:T(128)}, f32[64,4,8,128]{3,0,2,1:T(8,128)}, ...), condition=%wide.region_18.19_spmd.clone.clone, body=%wide.region_13.18_spmd.clone.clone.sunk | while | flops 135802880 | bytes 6869247 | solution.py:161
  187.8 3.2 conditional.26
  187.9 3.1 fusion.16
  194.5 3.0 conditional.27
  195.8 1.7 fusion.35
  282.9 2.5 bitcast_convert_fusion.1
  288.7 126.7 %while.67 = (s32[]{:T(128)}, f32[64,4,8,128]{3,0,2,1:T(8,128)}, f32[64,4,8,128]{3,0,2,1:T(8,128)S(1)}, f32[26,1,64,1024]{3,2,1,0:T(8,128)}, pred[26,1,2]{2,1,0:T...) while((s32[]{:T(128)}, f32[64,4,8,128]{3,0,2,1:T(8,128)}, ...), condition=%wide.region_24.25_spmd.clone.clone, body=%wide.region_19.24_spmd.clone.clone.sunk | while | flops 338636800 | bytes 28328468 | solution.py:220
  292.1 6.2 conditional.28
  302.6 7.9 %conditional.29 = ((f32[64,4,8,128]{3,0,2,1:T(8,128)S(1)}, f32[64,4,128]{2,0,1:T(8,128)S(1)}, f32[64,4,128]{2,0,1:T(8,128)S(1)})) conditional(s32[]{:T(128)} %bitcast.397, (f32[64,4,8,128]{3,0,2,1:T(8,128)S(1)}, f32[64,4,128]{2,0,1:T(8,128)S(1)}, f32[64,4,128]{2,0,1:T(8,128)S(1)}) %tuple.250, (pred[1,2]{1,0:T(4,128)(4,1)S(1)}, ...), branch_computations={%region_22.22_spmd, %region_23.23_spmd} | conditional | flops 169316352 | bytes 9162787 | solution.py:197
  415.4 3.6 bitcast_convert_fusion
  421.0 2.4 fusion.119
  423.4 1.6 copy.107
  425.1 2.3 convert_element_type.189
  429.6 11.1 %collective-permute-start.23 = (bf16[64,1024]{1,0:T(8,128)(2,1)S(1)}, bf16[64,1024]{1,0:T(8,128)(2,1)S(1)}, u32[]{:S(2)}, u32[]{:S(2)}) collective-permute-start(bf16[64,1024]{1,0:T(8,128)(2,1)S(1)} %slice_bitcast_fusion.11), channel_id=1, source_target_pairs={{8,0},{9,1},{10,2},{11,3},{12,4},{13,5},{14,6},{15,7},{24,16},{25,... | collective-permute-start | bytes 393224 | tf_op jit(solution)/shard_map/ppermute | solution.py:14
  440.8 68.8 %collective-permute-start.24 = (bf16[2,64,1024]{2,1,0:T(8,128)(2,1)S(1)}, bf16[2,64,1024]{2,1,0:T(8,128)(2,1)S(1)}, u32[]{:S(2)}, u32[]{:S(2)}) collective-permute-start(bf16[2,64,1024]{2,1,0:T(8,128)(2,1)S(1)} %copy-done.18), channel_id=1, source_target_pairs={{0,1},{1,2},{2,3},{3,4},{4,5},{5,6},{6,7},{7,8},{8,9},{9,10},{10,1... | collective-permute-start | bytes 786440 | tf_op jit(solution)/shard_map/ppermute | solution.py:14
  509.6 3.4 collective-permute-start.25
  513.0 1.9 collective-permute-start.26
  516.3 4.1 collective-permute-start.16
  521.5 107.5 %collective-permute-done.16 = bf16[64,1024]{1,0:T(8,128)(2,1)S(1)} collective-permute-done((bf16[64,1024]{1,0:T(8,128)(2,1)S(1)}, bf16[64,1024]{1,0:T(8,128)(2,1)S(1)}, u32[]{:S(2)}, u32[]{:S(2)}) %collective-permute-start.16) | collective-permute-done | bytes 131104 | tf_op jit(solution)/shard_map/ppermute | solution.py:14
  629.0 1.9 collective-permute-start.17
  631.9 5.5 collective-permute-done.17
  637.4 1.9 collective-permute-start.18
  640.3 5.1 collective-permute-done.18
  645.5 1.9 collective-permute-start.19
  648.4 3.9 collective-permute-done.19
  652.3 3.1 collective-permute-start.20
  655.4 4.6 collective-permute-done.20
  660.1 3.4 collective-permute-start.21
  663.5 5.8 collective-permute-done.21
  669.3 4.0 collective-permute-start.22
  673.4 3.0 collective-permute-start.27
  676.4 1.9 collective-permute-done.22
  678.3 2.1 collective-permute-start.28
  680.4 5.8 collective-permute-start.29
  686.2 1.9 collective-permute-start.30
  690.1 7.5 %collective-permute-done.29 = bf16[2,64,1024]{2,1,0:T(8,128)(2,1)S(1)} collective-permute-done((bf16[2,64,1024]{2,1,0:T(8,128)(2,1)S(1)}, bf16[2,64,1024]{2,1,0:T(8,128)(2,1)S(1)}, u32[]{:S(2)}, u32[]{:S(2)}) %collective-permute-start.29) | collective-permute-done | bytes 262176 | tf_op jit(solution)/shard_map/ppermute | solution.py:14
  697.6 1.6 collective-permute-done.30
  699.2 2.7 collective-permute-done.31
  (759 shorter events, 238.9 us)
Async XLA Ops:
  0.6 19.1 %copy-start.11 = (bf16[128,4096]{1,0:T(8,128)(2,1)S(1)}, bf16[128,4096]{1,0:T(8,128)(2,1)}, u32[]{:S(2)}) copy-start(bf16[128,4096]{1,0:T(8,128)(2,1)} %param.42) | copy-start | bytes 3145732
  2.6 50.4 %collective-permute-start.6 = (bf16[64,1024]{1,0:T(8,128)(2,1)S(1)}, bf16[64,1024]{1,0:T(8,128)(2,1)S(1)}, u32[]{:S(2)}, u32[]{:S(2)}) collective-permute-start(bf16[64,1024]{1,0:T(8,128)(2,1)S(1)} %slice.450), channel_id=1, source_target_pairs={{0,7},{1,8},{2,9},{3,10},{4,11},{5,12},{6,13},{7,14},{8,15},{16,23... | collective-permute-start | bytes 393224 | tf_op jit(solution)/shard_map/ppermute | solution.py:14
  8.0 43.0 %collective-permute-start.5 = (bf16[64,1024]{1,0:T(8,128)(2,1)S(1)}, bf16[64,1024]{1,0:T(8,128)(2,1)S(1)}, u32[]{:S(2)}, u32[]{:S(2)}) collective-permute-start(bf16[64,1024]{1,0:T(8,128)(2,1)S(1)} %slice.450), channel_id=1, source_target_pairs={{0,6},{1,7},{2,8},{3,9},{4,10},{5,11},{6,12},{7,13},{8,14},{9,15},... | collective-permute-start | bytes 393224 | tf_op jit(solution)/shard_map/ppermute | solution.py:14
  9.9 39.1 %collective-permute-start.4 = (bf16[64,1024]{1,0:T(8,128)(2,1)S(1)}, bf16[64,1024]{1,0:T(8,128)(2,1)S(1)}, u32[]{:S(2)}, u32[]{:S(2)}) collective-permute-start(bf16[64,1024]{1,0:T(8,128)(2,1)S(1)} %slice.450), channel_id=1, source_target_pairs={{0,5},{1,6},{2,7},{3,8},{4,9},{5,10},{6,11},{7,12},{8,13},{9,14},{... | collective-permute-start | bytes 393224 | tf_op jit(solution)/shard_map/ppermute | solution.py:14
  11.8 31.1 %collective-permute-start.3 = (bf16[64,1024]{1,0:T(8,128)(2,1)S(1)}, bf16[64,1024]{1,0:T(8,128)(2,1)S(1)}, u32[]{:S(2)}, u32[]{:S(2)}) collective-permute-start(bf16[64,1024]{1,0:T(8,128)(2,1)S(1)} %slice.450), channel_id=1, source_target_pairs={{0,4},{1,5},{2,6},{3,7},{4,8},{5,9},{6,10},{7,11},{8,12},{9,13},{1... | collective-permute-start | bytes 393224 | tf_op jit(solution)/shard_map/ppermute | solution.py:14
  13.8 10.8 %collective-permute-start = (bf16[64,1024]{1,0:T(8,128)(2,1)S(1)}, bf16[64,1024]{1,0:T(8,128)(2,1)S(1)}, u32[]{:S(2)}, u32[]{:S(2)}) collective-permute-start(bf16[64,1024]{1,0:T(8,128)(2,1)S(1)} %slice.450), channel_id=1, source_target_pairs={{0,1},{1,2},{2,3},{3,4},{4,5},{5,6},{6,7},{7,8},{8,9},{9,10},{10,1... | collective-permute-start | bytes 393224 | tf_op jit(solution)/shard_map/ppermute | solution.py:14
  19.3 2.3 copy-start.9
  20.0 63.4 %copy-start.3 = (bf16[16,8,32,128]{3,2,1,0:T(8,128)(2,1)}, bf16[16,8,32,128]{3,2,1,0:T(8,128)(2,1)S(1)}, u32[]{:S(2)}) copy-start(bf16[16,8,32,128]{3,2,1,0:T(8,128)(2,1)S(1)} %copy.175) | copy-start | bytes 3145732
  24.6 9.3 %collective-permute-start.1 = (bf16[64,1024]{1,0:T(8,128)(2,1)S(1)}, bf16[64,1024]{1,0:T(8,128)(2,1)S(1)}, u32[]{:S(2)}, u32[]{:S(2)}) collective-permute-start(bf16[64,1024]{1,0:T(8,128)(2,1)S(1)} %slice.450), channel_id=1, source_target_pairs={{0,2},{1,3},{2,4},{3,5},{4,6},{5,7},{6,8},{7,9},{8,10},{9,11},{10,... | collective-permute-start | bytes 393224 | tf_op jit(solution)/shard_map/ppermute | solution.py:14
  33.9 7.7 %collective-permute-start.2 = (bf16[64,1024]{1,0:T(8,128)(2,1)S(1)}, bf16[64,1024]{1,0:T(8,128)(2,1)S(1)}, u32[]{:S(2)}, u32[]{:S(2)}) collective-permute-start(bf16[64,1024]{1,0:T(8,128)(2,1)S(1)} %slice.450), channel_id=1, source_target_pairs={{0,3},{1,4},{2,5},{3,6},{4,7},{5,8},{6,9},{7,10},{8,11},{9,12},{10... | collective-permute-start | bytes 393224 | tf_op jit(solution)/shard_map/ppermute | solution.py:14
  41.6 15.3 %collective-permute-start.7 = (bf16[64,1024]{1,0:T(8,128)(2,1)S(1)}, bf16[64,1024]{1,0:T(8,128)(2,1)S(1)}, u32[]{:S(2)}, u32[]{:S(2)}) collective-permute-start(bf16[64,1024]{1,0:T(8,128)(2,1)S(1)} %slice.450), channel_id=1, source_target_pairs={{0,8},{1,9},{2,10},{3,11},{4,12},{5,13},{6,14},{7,15},{16,24},{17,... | collective-permute-start | bytes 393224 | tf_op jit(solution)/shard_map/ppermute | solution.py:14
  42.9 42.2 %collective-permute-start.15 = (bf16[2,64,1024]{2,1,0:T(8,128)(2,1)S(1)}, bf16[2,64,1024]{2,1,0:T(8,128)(2,1)S(1)}, u32[]{:S(2)}, u32[]{:S(2)}) collective-permute-start(bf16[2,64,1024]{2,1,0:T(8,128)(2,1)S(1)} %bitcast.420), channel_id=1, source_target_pairs={{8,0},{9,1},{10,2},{11,3},{12,4},{13,5},{14,6},{15,7},{24,16},{25,... | collective-permute-start | bytes 786440 | tf_op jit(solution)/shard_map/ppermute | solution.py:14
  49.0 36.0 %collective-permute-start.14 = (bf16[2,64,1024]{2,1,0:T(8,128)(2,1)S(1)}, bf16[2,64,1024]{2,1,0:T(8,128)(2,1)S(1)}, u32[]{:S(2)}, u32[]{:S(2)}) collective-permute-start(bf16[2,64,1024]{2,1,0:T(8,128)(2,1)S(1)} %bitcast.421), channel_id=1, source_target_pairs={{7,0},{8,1},{9,2},{10,3},{11,4},{12,5},{13,6},{14,7},{15,8},{23,16... | collective-permute-start | bytes 786440 | tf_op jit(solution)/shard_map/ppermute | solution.py:14
  51.0 22.2 %collective-permute-start.10 = (bf16[2,64,1024]{2,1,0:T(8,128)(2,1)S(1)}, bf16[2,64,1024]{2,1,0:T(8,128)(2,1)S(1)}, u32[]{:S(2)}, u32[]{:S(2)}) collective-permute-start(bf16[2,64,1024]{2,1,0:T(8,128)(2,1)S(1)} %bitcast.422), channel_id=1, source_target_pairs={{3,0},{4,1},{5,2},{6,3},{7,4},{8,5},{9,6},{10,7},{11,8},{12,9},{13... | collective-permute-start | bytes 786440 | tf_op jit(solution)/shard_map/ppermute | solution.py:14
  53.0 15.4 %collective-permute-start.8 = (bf16[2,64,1024]{2,1,0:T(8,128)(2,1)S(1)}, bf16[2,64,1024]{2,1,0:T(8,128)(2,1)S(1)}, u32[]{:S(2)}, u32[]{:S(2)}) collective-permute-start(bf16[2,64,1024]{2,1,0:T(8,128)(2,1)S(1)} %bitcast.423), channel_id=1, source_target_pairs={{1,0},{2,1},{3,2},{4,3},{5,4},{6,5},{7,6},{8,7},{9,8},{10,9},{11,1... | collective-permute-start | bytes 786440 | tf_op jit(solution)/shard_map/ppermute | solution.py:14
  56.9 13.4 %collective-permute-start.9 = (bf16[2,64,1024]{2,1,0:T(8,128)(2,1)S(1)}, bf16[2,64,1024]{2,1,0:T(8,128)(2,1)S(1)}, u32[]{:S(2)}, u32[]{:S(2)}) collective-permute-start(bf16[2,64,1024]{2,1,0:T(8,128)(2,1)S(1)} %bitcast.424), channel_id=1, source_target_pairs={{2,0},{3,1},{4,2},{5,3},{6,4},{7,5},{8,6},{9,7},{10,8},{11,9},{12,... | collective-permute-start | bytes 786440 | tf_op jit(solution)/shard_map/ppermute | solution.py:14
  68.4 12.3 %collective-permute-start.11 = (bf16[2,64,1024]{2,1,0:T(8,128)(2,1)S(1)}, bf16[2,64,1024]{2,1,0:T(8,128)(2,1)S(1)}, u32[]{:S(2)}, u32[]{:S(2)}) collective-permute-start(bf16[2,64,1024]{2,1,0:T(8,128)(2,1)S(1)} %bitcast.425), channel_id=1, source_target_pairs={{4,0},{5,1},{6,2},{7,3},{8,4},{9,5},{10,6},{11,7},{12,8},{13,9},{1... | collective-permute-start | bytes 786440 | tf_op jit(solution)/shard_map/ppermute | solution.py:14
  70.3 13.0 %collective-permute-start.12 = (bf16[2,64,1024]{2,1,0:T(8,128)(2,1)S(1)}, bf16[2,64,1024]{2,1,0:T(8,128)(2,1)S(1)}, u32[]{:S(2)}, u32[]{:S(2)}) collective-permute-start(bf16[2,64,1024]{2,1,0:T(8,128)(2,1)S(1)} %bitcast.426), channel_id=1, source_target_pairs={{5,0},{6,1},{7,2},{8,3},{9,4},{10,5},{11,6},{12,7},{13,8},{14,9},{... | collective-permute-start | bytes 786440 | tf_op jit(solution)/shard_map/ppermute | solution.py:14
  73.2 11.9 %collective-permute-start.13 = (bf16[2,64,1024]{2,1,0:T(8,128)(2,1)S(1)}, bf16[2,64,1024]{2,1,0:T(8,128)(2,1)S(1)}, u32[]{:S(2)}, u32[]{:S(2)}) collective-permute-start(bf16[2,64,1024]{2,1,0:T(8,128)(2,1)S(1)} %bitcast.427), channel_id=1, source_target_pairs={{6,0},{7,1},{8,2},{9,3},{10,4},{11,5},{12,6},{13,7},{14,8},{15,9},... | collective-permute-start | bytes 786440 | tf_op jit(solution)/shard_map/ppermute | solution.py:14
  85.1 1.8 copy-start.10
  282.9 2.5 copy-start.4
  293.6 0.6 copy-start.5
  293.6 2.4 copy-start.8
  294.2 2.7 copy-start
  295.7 1.2 copy-start.6
  297.3 1.0 copy-start.1
  415.4 5.0 slice-start
  415.4 5.6 slice-start.1
  421.0 2.4 copy-start.7
  423.4 3.9 copy-start.2
  427.6 13.2 %copy-start.18 = (bf16[2,64,1024]{2,1,0:T(8,128)(2,1)S(1)}, bf16[2,64,1024]{2,1,0:T(8,128)(2,1)}, u32[]{:S(2)}) copy-start(bf16[2,64,1024]{2,1,0:T(8,128)(2,1)} %get-tuple-element.864) | copy-start | bytes 786436
  427.6 82.0 %copy-start.17 = (bf16[2,64,1024]{2,1,0:T(8,128)(2,1)S(1)}, bf16[2,64,1024]{2,1,0:T(8,128)(2,1)}, u32[]{:S(2)}) copy-start(bf16[2,64,1024]{2,1,0:T(8,128)(2,1)} %get-tuple-element.865) | copy-start | bytes 786436
  427.6 85.4 %copy-start.16 = (bf16[2,64,1024]{2,1,0:T(8,128)(2,1)S(1)}, bf16[2,64,1024]{2,1,0:T(8,128)(2,1)}, u32[]{:S(2)}) copy-start(bf16[2,64,1024]{2,1,0:T(8,128)(2,1)} %get-tuple-element.866) | copy-start | bytes 786436
  429.6 243.7 %collective-permute-start.23 = (bf16[64,1024]{1,0:T(8,128)(2,1)S(1)}, bf16[64,1024]{1,0:T(8,128)(2,1)S(1)}, u32[]{:S(2)}, u32[]{:S(2)}) collective-permute-start(bf16[64,1024]{1,0:T(8,128)(2,1)S(1)} %slice_bitcast_fusion.11), channel_id=1, source_target_pairs={{8,0},{9,1},{10,2},{11,3},{12,4},{13,5},{14,6},{15,7},{24,16},{25,... | collective-permute-start | bytes 393224 | tf_op jit(solution)/shard_map/ppermute | solution.py:14
  440.8 239.5 %collective-permute-start.24 = (bf16[2,64,1024]{2,1,0:T(8,128)(2,1)S(1)}, bf16[2,64,1024]{2,1,0:T(8,128)(2,1)S(1)}, u32[]{:S(2)}, u32[]{:S(2)}) collective-permute-start(bf16[2,64,1024]{2,1,0:T(8,128)(2,1)S(1)} %copy-done.18), channel_id=1, source_target_pairs={{0,1},{1,2},{2,3},{3,4},{4,5},{5,6},{6,7},{7,8},{8,9},{9,10},{10,1... | collective-permute-start | bytes 786440 | tf_op jit(solution)/shard_map/ppermute | solution.py:14
  509.6 176.6 %collective-permute-start.25 = (bf16[2,64,1024]{2,1,0:T(8,128)(2,1)S(1)}, bf16[2,64,1024]{2,1,0:T(8,128)(2,1)S(1)}, u32[]{:S(2)}, u32[]{:S(2)}) collective-permute-start(bf16[2,64,1024]{2,1,0:T(8,128)(2,1)S(1)} %copy-done.17), channel_id=1, source_target_pairs={{0,2},{1,3},{2,4},{3,5},{4,6},{5,7},{6,8},{7,9},{8,10},{9,11},{10,... | collective-permute-start | bytes 786440 | tf_op jit(solution)/shard_map/ppermute | solution.py:14
  513.0 175.1 %collective-permute-start.26 = (bf16[2,64,1024]{2,1,0:T(8,128)(2,1)S(1)}, bf16[2,64,1024]{2,1,0:T(8,128)(2,1)S(1)}, u32[]{:S(2)}, u32[]{:S(2)}) collective-permute-start(bf16[2,64,1024]{2,1,0:T(8,128)(2,1)S(1)} %copy-done.16), channel_id=1, source_target_pairs={{0,3},{1,4},{2,5},{3,6},{4,7},{5,8},{6,9},{7,10},{8,11},{9,12},{10... | collective-permute-start | bytes 786440 | tf_op jit(solution)/shard_map/ppermute | solution.py:14
  516.3 157.1 %copy-start.15 = (bf16[2,64,1024]{2,1,0:T(8,128)(2,1)S(1)}, bf16[2,64,1024]{2,1,0:T(8,128)(2,1)}, u32[]{:S(2)}) copy-start(bf16[2,64,1024]{2,1,0:T(8,128)(2,1)} %get-tuple-element.867) | copy-start | bytes 786436
  516.3 162.0 %copy-start.14 = (bf16[2,64,1024]{2,1,0:T(8,128)(2,1)S(1)}, bf16[2,64,1024]{2,1,0:T(8,128)(2,1)}, u32[]{:S(2)}) copy-start(bf16[2,64,1024]{2,1,0:T(8,128)(2,1)} %get-tuple-element.868) | copy-start | bytes 786436
  516.3 164.1 %copy-start.13 = (bf16[2,64,1024]{2,1,0:T(8,128)(2,1)S(1)}, bf16[2,64,1024]{2,1,0:T(8,128)(2,1)}, u32[]{:S(2)}) copy-start(bf16[2,64,1024]{2,1,0:T(8,128)(2,1)} %get-tuple-element.869) | copy-start | bytes 786436
  516.3 169.9 %copy-start.12 = (bf16[2,64,1024]{2,1,0:T(8,128)(2,1)S(1)}, bf16[2,64,1024]{2,1,0:T(8,128)(2,1)}, u32[]{:S(2)}) copy-start(bf16[2,64,1024]{2,1,0:T(8,128)(2,1)} %get-tuple-element.870) | copy-start | bytes 786436
  516.3 112.7 %collective-permute-start.16 = (bf16[64,1024]{1,0:T(8,128)(2,1)S(1)}, bf16[64,1024]{1,0:T(8,128)(2,1)S(1)}, u32[]{:S(2)}, u32[]{:S(2)}) collective-permute-start(bf16[64,1024]{1,0:T(8,128)(2,1)S(1)} %get-tuple-element.878), channel_id=1, source_target_pairs={{1,0},{2,1},{3,2},{4,3},{5,4},{6,5},{7,6},{8,7},{9,8},{10,9},{11,1... | collective-permute-start | bytes 393224 | tf_op jit(solution)/shard_map/ppermute | solution.py:14
  629.0 8.4 %collective-permute-start.17 = (bf16[64,1024]{1,0:T(8,128)(2,1)S(1)}, bf16[64,1024]{1,0:T(8,128)(2,1)S(1)}, u32[]{:S(2)}, u32[]{:S(2)}) collective-permute-start(bf16[64,1024]{1,0:T(8,128)(2,1)S(1)} %get-tuple-element.877), channel_id=1, source_target_pairs={{2,0},{3,1},{4,2},{5,3},{6,4},{7,5},{8,6},{9,7},{10,8},{11,9},{12,... | collective-permute-start | bytes 393224 | tf_op jit(solution)/shard_map/ppermute | solution.py:14
  637.4 8.1 %collective-permute-start.18 = (bf16[64,1024]{1,0:T(8,128)(2,1)S(1)}, bf16[64,1024]{1,0:T(8,128)(2,1)S(1)}, u32[]{:S(2)}, u32[]{:S(2)}) collective-permute-start(bf16[64,1024]{1,0:T(8,128)(2,1)S(1)} %get-tuple-element.876), channel_id=1, source_target_pairs={{3,0},{4,1},{5,2},{6,3},{7,4},{8,5},{9,6},{10,7},{11,8},{12,9},{13... | collective-permute-start | bytes 393224 | tf_op jit(solution)/shard_map/ppermute | solution.py:14
  645.5 6.8 collective-permute-start.19
  652.3 7.7 %collective-permute-start.20 = (bf16[64,1024]{1,0:T(8,128)(2,1)S(1)}, bf16[64,1024]{1,0:T(8,128)(2,1)S(1)}, u32[]{:S(2)}, u32[]{:S(2)}) collective-permute-start(bf16[64,1024]{1,0:T(8,128)(2,1)S(1)} %get-tuple-element.874), channel_id=1, source_target_pairs={{5,0},{6,1},{7,2},{8,3},{9,4},{10,5},{11,6},{12,7},{13,8},{14,9},{... | collective-permute-start | bytes 393224 | tf_op jit(solution)/shard_map/ppermute | solution.py:14
  660.1 9.3 %collective-permute-start.21 = (bf16[64,1024]{1,0:T(8,128)(2,1)S(1)}, bf16[64,1024]{1,0:T(8,128)(2,1)S(1)}, u32[]{:S(2)}, u32[]{:S(2)}) collective-permute-start(bf16[64,1024]{1,0:T(8,128)(2,1)S(1)} %get-tuple-element.873), channel_id=1, source_target_pairs={{6,0},{7,1},{8,2},{9,3},{10,4},{11,5},{12,6},{13,7},{14,8},{15,9},... | collective-permute-start | bytes 393224 | tf_op jit(solution)/shard_map/ppermute | solution.py:14
  669.3 9.0 %collective-permute-start.22 = (bf16[64,1024]{1,0:T(8,128)(2,1)S(1)}, bf16[64,1024]{1,0:T(8,128)(2,1)S(1)}, u32[]{:S(2)}, u32[]{:S(2)}) collective-permute-start(bf16[64,1024]{1,0:T(8,128)(2,1)S(1)} %get-tuple-element.872), channel_id=1, source_target_pairs={{7,0},{8,1},{9,2},{10,3},{11,4},{12,5},{13,6},{14,7},{15,8},{23,16... | collective-permute-start | bytes 393224 | tf_op jit(solution)/shard_map/ppermute | solution.py:14
  673.4 16.2 %collective-permute-start.27 = (bf16[2,64,1024]{2,1,0:T(8,128)(2,1)S(1)}, bf16[2,64,1024]{2,1,0:T(8,128)(2,1)S(1)}, u32[]{:S(2)}, u32[]{:S(2)}) collective-permute-start(bf16[2,64,1024]{2,1,0:T(8,128)(2,1)S(1)} %copy-done.15), channel_id=1, source_target_pairs={{0,4},{1,5},{2,6},{3,7},{4,8},{5,9},{6,10},{7,11},{8,12},{9,13},{1... | collective-permute-start | bytes 786440 | tf_op jit(solution)/shard_map/ppermute | solution.py:14
  678.3 11.9 %collective-permute-start.28 = (bf16[2,64,1024]{2,1,0:T(8,128)(2,1)S(1)}, bf16[2,64,1024]{2,1,0:T(8,128)(2,1)S(1)}, u32[]{:S(2)}, u32[]{:S(2)}) collective-permute-start(bf16[2,64,1024]{2,1,0:T(8,128)(2,1)S(1)} %copy-done.14), channel_id=1, source_target_pairs={{0,5},{1,6},{2,7},{3,8},{4,9},{5,10},{6,11},{7,12},{8,13},{9,14},{... | collective-permute-start | bytes 786440 | tf_op jit(solution)/shard_map/ppermute | solution.py:14
  680.4 17.2 %collective-permute-start.29 = (bf16[2,64,1024]{2,1,0:T(8,128)(2,1)S(1)}, bf16[2,64,1024]{2,1,0:T(8,128)(2,1)S(1)}, u32[]{:S(2)}, u32[]{:S(2)}) collective-permute-start(bf16[2,64,1024]{2,1,0:T(8,128)(2,1)S(1)} %copy-done.13), channel_id=1, source_target_pairs={{0,6},{1,7},{2,8},{3,9},{4,10},{5,11},{6,12},{7,13},{8,14},{9,15},... | collective-permute-start | bytes 786440 | tf_op jit(solution)/shard_map/ppermute | solution.py:14
  686.2 12.9 %collective-permute-start.30 = (bf16[2,64,1024]{2,1,0:T(8,128)(2,1)S(1)}, bf16[2,64,1024]{2,1,0:T(8,128)(2,1)S(1)}, u32[]{:S(2)}, u32[]{:S(2)}) collective-permute-start(bf16[2,64,1024]{2,1,0:T(8,128)(2,1)S(1)} %copy-done.12), channel_id=1, source_target_pairs={{0,7},{1,8},{2,9},{3,10},{4,11},{5,12},{6,13},{7,14},{8,15},{16,23... | collective-permute-start | bytes 786440 | tf_op jit(solution)/shard_map/ppermute | solution.py:14
  688.2 13.7 %collective-permute-start.31 = (bf16[2,64,1024]{2,1,0:T(8,128)(2,1)S(1)}, bf16[2,64,1024]{2,1,0:T(8,128)(2,1)S(1)}, u32[]{:S(2)}, u32[]{:S(2)}) collective-permute-start(bf16[2,64,1024]{2,1,0:T(8,128)(2,1)S(1)} %get-tuple-element.871), channel_id=1, source_target_pairs={{0,8},{1,9},{2,10},{3,11},{4,12},{5,13},{6,14},{7,15},{16,24},{17,... | collective-permute-start | bytes 786440 | tf_op jit(solution)/shard_map/ppermute | solution.py:14
where the time goes:
time: 711 us; the launch traced here: 703 us
  local copies, waits for them, and re-layouts  200 us (28%)
  waiting for transfers between devices  181 us (25%)
  starting transfers between devices  161 us (23%)
  loops' own time  108 us (15%)
  other arithmetic  39.1 us (5%)
  matrix products  12 us (2%)
    ppermute x32, waiting for transfers between devices, shifted(): return lax.ppermute(x, axis, pairs)  181 us
    ppermute x32, starting transfers between devices, shifted(): return lax.ppermute(x, axis, pairs)  161 us
    squeeze x78, local copies, waits for them, and re-layouts, local(): final_stats = lax.scan(stats_turn, start_stats, stacked)[0]  51.2 us
    another operation x1, loops' own time, local(): final_stats = lax.scan(stats_turn, start_stats, stacked)[0]  34.9 us
    another operation x1, loops' own time, local(): query_grads, partials = lax.scan(grad_turn, start_grads, stacked)  34.9 us
    another operation x1, loops' own time, local(): final_out = lax.scan(out_turn, start_out, stacked)[0]  34.9 us
    squeeze x26, local copies, waits for them, and re-layouts, stats_turn(): kv_turn[0]  23.9 us
    squeeze x26, local copies, waits for them, and re-layouts, out_turn(): kv_turn[0]  23.9 us
  transfers between devices with their start and end apart: 32, of which 18 were waited for; matrix products, arithmetic and copies ran while one was open for 2% of the time, Pallas kernels for 0%

commit v1 on v0

v1 whole, which is shorter than its diff:
```python
import functools

import jax
import jax.numpy as jnp
from jax import lax
from jax.experimental import pallas as pl
from jax.experimental.pallas import tpu as pltpu
from jax.sharding import PartitionSpec as P

HEADS = 32
KV_HEADS = 4
HEAD_DIM = 128
GROUPS = HEADS // KV_HEADS
STRETCH = 64
REACH = 8
WINDOW = (REACH + 1) * STRETCH
ROWS = GROUPS * STRETCH
PAIR = 2 * HEAD_DIM
MESH = pl.DeviceIdType.MESH
SCALE = HEAD_DIM ** (-0.5)
SCALE_LOG2E = SCALE * 1.4426950408889634


def dot_nt(a, b):
    return lax.dot_general(a, b, (((1,), (1,)), ((), ())), preferred_element_type=jnp.float32)


def dot_nn(a, b):
    return lax.dot_general(a, b, (((1,), (0,)), ((), ())), preferred_element_type=jnp.float32)


def when_copy(active, remote, source, target, send_sem, recv_sem, device):
    @pl.when(active & remote)
    def _():
        pltpu.make_async_remote_copy(
            source, target, send_sem, recv_sem, device_id={"ctx": device}, device_id_type=MESH
        ).start()

    @pl.when(active & jnp.logical_not(remote))
    def _():
        pltpu.make_async_copy(source, target, recv_sem).start()


def kernel(
    n, docs_ref, q_ref, k_ref, v_ref, do_ref, o_ref, dq_ref, dk_ref, dv_ref,
    own, win, part, recv, diag, s_ref, dp_ref, p_ref, ds_ref,
    gsend, grecv, rsend, rrecv,
):
    me = lax.axis_index("ctx")
    last = 2 * n - 1

    barrier = pltpu.get_barrier_semaphore()

    @pl.loop(1, n)
    def _(step):
        pl.semaphore_signal(
            barrier, inc=1, device_id={"ctx": lax.rem(me + step, n)}, device_id_type=MESH
        )

    for g in range(KV_HEADS):
        cols = slice(g * HEAD_DIM, (g + 1) * HEAD_DIM)
        for o in range(2):
            rows = slice(o * STRETCH, (o + 1) * STRETCH)
            own[g, o, :, :HEAD_DIM] = k_ref[rows, cols]
            own[g, o, :, HEAD_DIM:] = v_ref[rows, cols]
            win[g, o, REACH * STRETCH :, :HEAD_DIM] = k_ref[rows, cols]
            win[g, o, REACH * STRETCH :, HEAD_DIM:] = v_ref[rows, cols]

    @pl.loop(0, KV_HEADS * REACH)
    def _(turn):
        g, k = turn // REACH, lax.rem(turn, REACH) + 1

        @pl.when(me < k)
        def _():
            row = pl.multiple_of((REACH - k) * STRETCH, STRETCH)
            win[g, 0, pl.ds(row, STRETCH), :] = jnp.zeros((STRETCH, PAIR), jnp.bfloat16)
            recv[g, 1, k - 1] = jnp.zeros((STRETCH, PAIR), jnp.bfloat16)

    pl.semaphore_wait(barrier, n - 1)

    @pl.loop(0, KV_HEADS * REACH)
    def _(turn):
        g, k = turn // REACH, lax.rem(turn, REACH) + 1
        row = pl.multiple_of((REACH - k) * STRETCH, STRETCH)
        low = me + k < n
        reader = jnp.where(low, me + k, last - me - k)
        slot = jnp.where(low, 0, 1)
        when_copy(
            k >= 1, reader != me, own.at[g, 0], win.at[g, slot, pl.ds(row, STRETCH)],
            gsend.at[g, 0, k - 1], grecv.at[g, slot, k - 1], reader,
        )

        @pl.when(me >= k)
        def _():
            pltpu.make_async_remote_copy(
                own.at[g, 1], win.at[g, 1, pl.ds(row, STRETCH)], gsend.at[g, 1, k - 1],
                grecv.at[g, 1, k - 1], device_id={"ctx": me - k}, device_id_type=MESH,
            ).start()

    def doc_start(block):
        end = jnp.int32(0)
        start = jnp.int32(0)
        for d in range(8):
            end = end + docs_ref[d]
            start = jnp.where(end <= block, end, start)
        return start

    col = lax.broadcasted_iota(jnp.int32, (STRETCH, ROWS), 0)
    row_of = lax.rem(lax.broadcasted_iota(jnp.int32, (STRETCH, ROWS), 1), STRETCH)
    later = row_of < col

    def eights(x, op):
        return op(x.reshape(STRETCH // 8, 8, ROWS), axis=0)

    def head_rows(ref, o, g):
        r = pl.multiple_of(o * STRETCH, STRETCH)
        return jnp.concatenate(
            [
                ref[
                    pl.ds(r, STRETCH),
                    pl.ds(pl.multiple_of((g * GROUPS + h) * HEAD_DIM, HEAD_DIM), HEAD_DIM),
                ]
                for h in range(GROUPS)
            ],
            axis=0,
        )

    def put_heads(ref, o, g, value):
        r = pl.multiple_of(o * STRETCH, STRETCH)
        for h in range(GROUPS):
            ref[
                pl.ds(r, STRETCH),
                pl.ds(pl.multiple_of((g * GROUPS + h) * HEAD_DIM, HEAD_DIM), HEAD_DIM),
            ] = value[h * STRETCH : (h + 1) * STRETCH]

    def tile(g, o):
        block = jnp.where(o == 0, me, last - me)
        start = doc_start(block)
        bias = [
            jnp.where(block - (REACH - kb) >= start, jnp.float32(0), jnp.float32(-jnp.inf))
            for kb in range(REACH + 1)
        ]
        q = head_rows(q_ref, o, g)
        do = head_rows(do_ref, o, g)
        keys = win[g, o, :, :HEAD_DIM]
        vals = win[g, o, :, HEAD_DIM:]
        s_ref[...] = dot_nt(keys, q)
        dp_ref[...] = dot_nt(vals, do)
        spans = [slice(kb * STRETCH, (kb + 1) * STRETCH) for kb in range(REACH + 1)]
        on_diag = jnp.where(later, -jnp.inf, s_ref[spans[REACH], :])
        s_ref[spans[REACH], :] = on_diag
        top = eights(on_diag, jnp.max)
        for kb in range(REACH):
            top = jnp.maximum(top, eights(s_ref[spans[kb], :], jnp.max) + bias[kb])
        top = jnp.max(top, axis=0, keepdims=True) * SCALE_LOG2E
        total = jnp.zeros((8, ROWS), jnp.float32)
        inner = jnp.zeros((8, ROWS), jnp.float32)
        for kb in range(REACH + 1):
            e = jnp.exp2(s_ref[spans[kb], :] * SCALE_LOG2E + (bias[kb] - top))
            s_ref[spans[kb], :] = e
            total = total + eights(e, jnp.sum)
            inner = inner + eights(e * dp_ref[spans[kb], :], jnp.sum)
        inverse = 1.0 / jnp.sum(total, axis=0, keepdims=True)
        inner = jnp.sum(inner, axis=0, keepdims=True) * inverse
        for kb in range(REACH + 1):
            p = s_ref[spans[kb], :] * inverse
            p_ref[spans[kb], :] = p.astype(jnp.bfloat16)
            ds_ref[spans[kb], :] = (p * (dp_ref[spans[kb], :] - inner)).astype(jnp.bfloat16)
        put_heads(o_ref, o, g, dot_nn(vals.T, p_ref[...]).astype(jnp.bfloat16).T)
        put_heads(dq_ref, o, g, (SCALE * dot_nn(keys.T, ds_ref[...])).astype(jnp.bfloat16).T)
        dv = dot_nn(p_ref[...], do)
        dk = SCALE * dot_nn(ds_ref[...], q)
        edge = REACH * STRETCH
        part[g, o, :, :HEAD_DIM] = dk[:edge].astype(jnp.bfloat16)
        part[g, o, :, HEAD_DIM:] = dv[:edge].astype(jnp.bfloat16)
        diag[g, o, :, :HEAD_DIM] = dk[edge:]
        diag[g, o, :, HEAD_DIM:] = dv[edge:]

    def gather_wait(g, o, k):
        row = pl.multiple_of((REACH - k) * STRETCH, STRETCH)
        here = pltpu.make_async_copy(
            own.at[g, o], win.at[g, o, pl.ds(row, STRETCH)], grecv.at[g, o, k - 1]
        )

        @pl.when((o == 1) | (me >= k))
        def _():
            here.wait()

    @pl.loop(0, KV_HEADS)
    def _(g):
        @pl.loop(0, 2)
        def _(o):
            @pl.loop(1, REACH + 1)
            def _(k):
                gather_wait(g, o, k)

            tile(g, o)

            @pl.loop(1, REACH + 1)
            def _(k):
                row = pl.multiple_of((REACH - k) * STRETCH, STRETCH)
                high = (o == 1) & (me + k < n)
                home = jnp.where(o == 0, me - k, jnp.where(high, me + k, last - me - k))
                slot = jnp.where(high, 1, 0)
                when_copy(
                    home >= 0, home != me, part.at[g, o, pl.ds(row, STRETCH)],
                    recv.at[g, slot, k - 1], rsend.at[g, o, k - 1], rrecv.at[g, slot, k - 1],
                    home,
                )

    @pl.loop(0, KV_HEADS)
    def _(g):
        cols = pl.ds(pl.multiple_of(g * HEAD_DIM, HEAD_DIM), HEAD_DIM)
        for o in range(2):

            @pl.loop(1, REACH + 1)
            def _(k):
                @pl.when((o == 0) | (me >= k))
                def _():
                    pltpu.make_async_copy(
                        part.at[g, o, pl.ds(0, STRETCH)], recv.at[g, o, k - 1],
                        rrecv.at[g, o, k - 1],
                    ).wait()

            rows = slice(o * STRETCH, (o + 1) * STRETCH)
            acc = diag[g, o]
            for k in range(REACH):
                acc = acc + recv[g, o, k].astype(jnp.float32)
            dk_ref[rows, cols] = acc[:, :HEAD_DIM].astype(jnp.bfloat16)
            dv_ref[rows, cols] = acc[:, HEAD_DIM:].astype(jnp.bfloat16)

    @pl.loop(0, KV_HEADS * REACH)
    def _(turn):
        g, k = turn // REACH, lax.rem(turn, REACH) + 1
        low = me + k < n
        reader = jnp.where(low, me + k, last - me - k)

        @pl.when(reader != me)
        def _():
            pltpu.make_async_copy(own.at[g, 0], own.at[g, 0], gsend.at[g, 0, k - 1]).wait()

        @pl.when(me >= k)
        def _():
            pltpu.make_async_copy(own.at[g, 1], own.at[g, 1], gsend.at[g, 1, k - 1]).wait()
            pltpu.make_async_copy(own.at[g, 0], own.at[g, 0], rsend.at[g, 0, k - 1]).wait()

        @pl.when(last - me - k != me)
        def _():
            pltpu.make_async_copy(own.at[g, 1], own.at[g, 1], rsend.at[g, 1, k - 1]).wait()


def local(queries, keys, values, grad_out, doc_blocks):
    n = lax.axis_size("ctx")
    vmem = pl.BlockSpec(memory_space=pltpu.VMEM)
    bf16, f32 = jnp.bfloat16, jnp.float32
    dma = pltpu.SemaphoreType.DMA((KV_HEADS, 2, REACH))
    return pl.pallas_call(
        functools.partial(kernel, n),
        out_shape=(
            jax.ShapeDtypeStruct(queries.shape, bf16),
            jax.ShapeDtypeStruct(queries.shape, bf16),
            jax.ShapeDtypeStruct(keys.shape, bf16),
            jax.ShapeDtypeStruct(values.shape, bf16),
        ),
        in_specs=[pl.BlockSpec(memory_space=pltpu.SMEM)] + [vmem] * 4,
        out_specs=(vmem,) * 4,
        scratch_shapes=[
            pltpu.VMEM((KV_HEADS, 2, STRETCH, PAIR), bf16),
            pltpu.VMEM((KV_HEADS, 2, WINDOW, PAIR), bf16),
            pltpu.VMEM((KV_HEADS, 2, REACH * STRETCH, PAIR), bf16),
            pltpu.VMEM((KV_HEADS, 2, REACH, STRETCH, PAIR), bf16),
            pltpu.VMEM((KV_HEADS, 2, STRETCH, PAIR), f32),
            pltpu.VMEM((WINDOW, ROWS), f32),
            pltpu.VMEM((WINDOW, ROWS), f32),
            pltpu.VMEM((WINDOW, ROWS), bf16),
            pltpu.VMEM((WINDOW, ROWS), bf16),
            dma, dma, dma, dma,
        ],
        compiler_params=pltpu.CompilerParams(
            collective_id=0, has_side_effects=True, vmem_limit_bytes=48 * 2**20
        ),
    )(doc_blocks, queries, keys, values, grad_out)


def solution(mesh):
    token = P(("dp", "ctx"), None)
    return jax.shard_map(
        local, mesh=mesh, in_specs=(token, token, token, token, P("dp")),
        out_specs=(token,) * 4, check_vma=False,
    )
```

time: 711 us -> 88.5 us (0.12)
  the two profiles are of different devices: /device:TPU:464 before, /device:TPU:218 now
where the time goes in v1:
time: 88.5 us; the launch traced here: 88.3 us
  Pallas kernels  79.4 us (90%)
  local copies, waits for them, and re-layouts  8.16 us (9%)
    pallas_call x1, Pallas kernels, local(): pl.pallas_call(functools.partial(kernel, n), out_shape=(jax.ShapeDtypeStr...  79.4 us
    unnamed x14, local copies, waits for them, and re-layouts  8.16 us

profile of v1, /device:TPU:218, one launch (start us, length us, event | category | flops | bytes accessed | tf_op | source)
XLA Modules:
  0.0 88.3 jit_solution(16263313704092105072)
XLA Ops:
  0.6 0.0 copy-start
  0.6 1.2 %copy-done = bf16[128,4096]{1,0:T(8,128)(2,1)S(1)} copy-done((bf16[128,4096]{1,0:T(8,128)(2,1)S(1)}, bf16[128,4096]{1,0:T(8,128)(2,1)}, u32[]{:S(2)}) %copy-start) | copy-done | bytes 1048600
  1.9 0.0 copy-start.1
  1.9 1.2 %copy-done.1 = bf16[128,4096]{1,0:T(8,128)(2,1)S(1)} copy-done((bf16[128,4096]{1,0:T(8,128)(2,1)S(1)}, bf16[128,4096]{1,0:T(8,128)(2,1)}, u32[]{:S(2)}) %copy-start.1) | copy-done | bytes 1048600
  3.1 0.0 copy-start.2
  3.1 0.9 %copy-done.2 = bf16[128,512]{1,0:T(8,128)(2,1)S(1)} copy-done((bf16[128,512]{1,0:T(8,128)(2,1)S(1)}, bf16[128,512]{1,0:T(8,128)(2,1)}, u32[]{:S(2)}) %copy-start.2) | copy-done | bytes 131096
  4.0 0.0 copy-start.3
  4.0 0.9 %copy-done.3 = bf16[128,512]{1,0:T(8,128)(2,1)S(1)} copy-done((bf16[128,512]{1,0:T(8,128)(2,1)S(1)}, bf16[128,512]{1,0:T(8,128)(2,1)}, u32[]{:S(2)}) %copy-start.3) | copy-done | bytes 131096
  4.9 0.0 copy-start.4
  4.9 0.7 copy-done.4
  5.5 79.4 %shard_map.84 = (bf16[128,4096]{1,0:T(8,128)(2,1)S(1)}, bf16[128,4096]{1,0:T(8,128)(2,1)S(1)}, bf16[128,512]{1,0:T(8,128)(2,1)S(1)}, bf16[128,512]{1,0:T(8,128)(2,1)S(1)}) custom-call(s32[8]{0:T(128)S(1)} %copy-done.4, bf16[128,4096]{1,0:T(8,128)(2,1)S(1)} %copy-done, bf16[128,512]{1,0:T(8,128)(2,1)S(1)} %copy-done.2, bf16[128,512]{1,0:T(8,128)(2,1)S(1)} %copy-done.3, ...), custom_call_target="tpu_custom_call" | custom-call | tf_op jit(solution)/shard_map/pallas_call | solution.py:257
  85.0 1.0 %copy.13 = bf16[128,4096]{1,0:T(8,128)(2,1)} copy(bf16[128,4096]{1,0:T(8,128)(2,1)S(1)} %get-tuple-element.8) | data formatting | bytes 2097152
  86.0 1.0 %copy.14 = bf16[128,4096]{1,0:T(8,128)(2,1)} copy(bf16[128,4096]{1,0:T(8,128)(2,1)S(1)} %get-tuple-element.9) | data formatting | bytes 2097152
  86.9 0.7 copy.15
  87.6 0.7 copy.16
Async XLA Ops:
  0.6 1.2 %copy-start = (bf16[128,4096]{1,0:T(8,128)(2,1)S(1)}, bf16[128,4096]{1,0:T(8,128)(2,1)}, u32[]{:S(2)}) copy-start(bf16[128,4096]{1,0:T(8,128)(2,1)} %q_ref.1) | copy-start | bytes 3145732
  1.9 1.2 %copy-start.1 = (bf16[128,4096]{1,0:T(8,128)(2,1)S(1)}, bf16[128,4096]{1,0:T(8,128)(2,1)}, u32[]{:S(2)}) copy-start(bf16[128,4096]{1,0:T(8,128)(2,1)} %do_ref.1) | copy-start | bytes 3145732
  3.1 0.9 %copy-start.2 = (bf16[128,512]{1,0:T(8,128)(2,1)S(1)}, bf16[128,512]{1,0:T(8,128)(2,1)}, u32[]{:S(2)}) copy-start(bf16[128,512]{1,0:T(8,128)(2,1)} %k_ref.1) | copy-start | bytes 393220
  4.0 0.9 %copy-start.3 = (bf16[128,512]{1,0:T(8,128)(2,1)S(1)}, bf16[128,512]{1,0:T(8,128)(2,1)}, u32[]{:S(2)}) copy-start(bf16[128,512]{1,0:T(8,128)(2,1)} %v_ref.1) | copy-start | bytes 393220
  4.9 0.7 copy-start.4

commit v2 on v1

v2 whole, which is shorter than its diff:
```python
import jax
import jax.numpy as jnp
from jax import lax
from jax.experimental import pallas as pl
from jax.experimental.pallas import tpu as pltpu
from jax.sharding import PartitionSpec as P

HEADS = 32
KV_HEADS = 4
HEAD_DIM = 128
GROUPS = HEADS // KV_HEADS
STRETCH = 64
REACH = 8
WINDOW = (REACH + 1) * STRETCH
ROWS = GROUPS * STRETCH
PAIR = 2 * HEAD_DIM
MESH = pl.DeviceIdType.MESH
SCALE = HEAD_DIM ** (-0.5)
SCALE_LOG2E = SCALE * 1.4426950408889634


def dot_nt(a, b):
    return lax.dot_general(a, b, (((1,), (1,)), ((), ())), preferred_element_type=jnp.float32)


def dot_nn(a, b):
    return lax.dot_general(a, b, (((1,), (0,)), ((), ())), preferred_element_type=jnp.float32)


N, LAST, DEPTH = 16, 31, 3

TREE = (
    (0, 0, 0, 0, 1, 2, 6, 0,),
    (3, 1, 5, 1, 2, 3, 4, 1,),
    (2, 6, 6, 2, 4, 10, 5, 2,),
    (7, 4, 7, 3, 4, 11, 6, 7,),
    (4, 5, 4, 4, 5, 6, 8, 4,),
    (7, 5, 9, 5, 6, 8, 8, 5,),
    (6, 10, 8, 6, 7, 8, 14, 10,),
    (12, 11, 14, 7, 15, 9, 15, 7,),
    (8, 9, 8, 8, 12, 10, 11,),
    (9, 10, 13, 9, 13, 12,),
    (10, 13, 14, 10, 14,),
    (15, 14, 15, 11,),
    (15, 12, 12, 12,),
    (14, 15, 13, 13, 14,),
    (13, 14, 15, 13, 14, 14,),
    (12, 13, 11, 15, 15, 12, 15,),
    (15, 12, 13, 9, 7, 15, 15, 13,),
    (10, 11, 11, 10, 14, 10, 14, 9,),
    (9, 5, 11, 9, 13, 11, 9, 8,),
    (8, 9, 10, 11, 12, 8, 8, 8,),
    (7, 7, 6, 7, 11, 4, 10, 11,),
    (6, 7, 8, 6, 10, 6, 10, 5,),
    (9, 6, 1, 8, 9, 5, 3, 9,),
    (8, 0, 6, 7, 8, 1, 4, 4,),
    (3, 5, 3, 7, 7, 4, 2,),
    (4, 2, 6, 2, 5, 6,),
    (3, 5, 1, 1, 5,),
    (4, 0, 1, 0,),
    (3, 2, 3,),
    (1, 2,),
    (1,),
    (),
)


def holder(block):
    return min(block, LAST - block)


def place(device, block):
    if block in (device, LAST - device):
        return (0, 0) if block == device else (1, 0)
    low = device - block
    return (0, low) if 0 < low <= REACH else (1, LAST - device - block)


class Slot:
    def __init__(self, device, block, level):
        self.o, self.k = place(device, block)
        self.level, self.to, self.source = level, [], None


def build():
    plan = [[] for _ in range(N)]
    count = [0] * N
    for block, parents in enumerate(TREE):
        top = min(block + REACH, LAST)
        readers = sorted({holder(b) for b in range(block + 1, top + 1)} - {holder(block)})
        slots = {holder(block): Slot(holder(block), block, 0)}
        left = dict(zip(readers, parents, strict=True))
        while left:
            for device, source in sorted(left.items()):
                if source in slots and device not in slots and slots[source].level < DEPTH:
                    slots[device] = Slot(device, block, slots[source].level + 1)
                    slots[device].source = (source, count[source])
                    slots[source].to.append((device, count[source], slots[device]))
                    count[source] += 1
                    del left[device]
        for device, slot in slots.items():
            plan[device].append(slot)
    return plan, max(count)


PLAN, HOPS = build()
NEAR = [
    sorted(
        {hop[0] for slot in slots for hop in slot.to}
        | {slot.source[0] for slot in slots if slot.source}
    )
    for slots in PLAN
]


def each_device(me, emit):
    for device in range(N):

        @pl.when(me == device)
        def _():
            emit(device)


def span(k):
    return slice((REACH - k) * STRETCH, (REACH - k + 1) * STRETCH)


def kernel(
    docs_hbm, q_hbm, k_hbm, v_hbm, do_hbm, o_hbm, dq_hbm, dk_hbm, dv_hbm,
    docs, q_buf, k_buf, v_buf, do_buf, o_buf, dq_buf, dk_buf, dv_buf, win, part, diag, coming,
    s_ref, dp_ref, p_ref, ds_ref, fetch, store, keep, gsend, grecv, rsend, rrecv,
):
    me = lax.axis_index("ctx")
    last = LAST

    fetches = [
        pltpu.make_async_copy(a, b, fetch.at[i])
        for i, (a, b) in enumerate(
            [(k_hbm, k_buf), (v_hbm, v_buf), (docs_hbm, docs), (q_hbm, q_buf), (do_hbm, do_buf)]
        )
    ]
    for copy in fetches:
        copy.start()

    barrier = pltpu.get_barrier_semaphore()

    def greet(device):
        for near in NEAR[device]:
            pl.semaphore_signal(barrier, inc=1, device_id={"ctx": near}, device_id_type=MESH)

    each_device(me, greet)
    fetches[0].wait()
    fetches[1].wait()
    for g in range(KV_HEADS):
        cols = slice(g * HEAD_DIM, (g + 1) * HEAD_DIM)
        for o in range(2):
            rows = slice(o * STRETCH, (o + 1) * STRETCH)
            win[g, o, span(0), :HEAD_DIM] = k_buf[rows, cols]
            win[g, o, span(0), HEAD_DIM:] = v_buf[rows, cols]

    @pl.loop(0, KV_HEADS)
    def _(g):
        for k in range(1, REACH + 1):

            @pl.when(me < k)
            def _():
                win[g, 0, span(k), :] = jnp.zeros((STRETCH, PAIR), jnp.bfloat16)

    each_device(me, lambda device: pl.semaphore_wait(barrier, len(NEAR[device])))

    def arrived(g, slot):
        here = win.at[g, slot.o, span(slot.k)]
        pltpu.make_async_copy(here, here, grecv.at[g, slot.o, slot.k - 1]).wait()

    def spread(level, g):
        def emit(device):
            for slot in PLAN[device]:
                if slot.level != level or not slot.to:
                    continue
                if slot.k:
                    arrived(g, slot)
                for there, e, other in slot.to:
                    pltpu.make_async_remote_copy(
                        win.at[g, slot.o, span(slot.k)], win.at[g, other.o, span(other.k)],
                        gsend.at[g, e], grecv.at[g, other.o, other.k - 1],
                        device_id={"ctx": there}, device_id_type=MESH,
                    ).start()

        each_device(me, emit)

    def twins(device):
        base = last - 2 * device
        return [(k, k + base) for k in range(REACH + 1) if k <= device and k + base <= REACH]

    def complete(g):
        def emit(device):
            for slot in PLAN[device]:
                if slot.k and not slot.to:
                    arrived(g, slot)
            for low, high in twins(device):
                win[g, 1, span(high), :] = win[g, 0, span(low), :]

        each_device(me, emit)

    def doc_start(block):
        end = jnp.int32(0)
        start = jnp.int32(0)
        for d in range(8):
            end = end + docs[d]
            start = jnp.where(end <= block, end, start)
        return start

    col = lax.broadcasted_iota(jnp.int32, (STRETCH, ROWS), 0)
    row_of = lax.rem(lax.broadcasted_iota(jnp.int32, (STRETCH, ROWS), 1), STRETCH)
    later = row_of < col

    def eights(x, op):
        return op(x.reshape(STRETCH // 8, 8, ROWS), axis=0)

    def head_rows(ref, o, g):
        r = pl.multiple_of(o * STRETCH, STRETCH)
        return jnp.concatenate(
            [
                ref[
                    pl.ds(r, STRETCH),
                    pl.ds(pl.multiple_of((g * GROUPS + h) * HEAD_DIM, HEAD_DIM), HEAD_DIM),
                ]
                for h in range(GROUPS)
            ],
            axis=0,
        )

    def put_heads(ref, o, g, value):
        r = pl.multiple_of(o * STRETCH, STRETCH)
        for h in range(GROUPS):
            ref[
                pl.ds(r, STRETCH),
                pl.ds(pl.multiple_of((g * GROUPS + h) * HEAD_DIM, HEAD_DIM), HEAD_DIM),
            ] = value[h * STRETCH : (h + 1) * STRETCH]

    def stores(g, o):
        rows = pl.ds(pl.multiple_of(o * STRETCH, STRETCH), STRETCH)
        width = GROUPS * HEAD_DIM
        cols = pl.ds(pl.multiple_of(g * width, width), width)
        return [
            pltpu.make_async_copy(a.at[rows, cols], b.at[rows, cols], store.at[i, g, o])
            for i, (a, b) in enumerate([(o_buf, o_hbm), (dq_buf, dq_hbm)])
        ]

    def keeps(g):
        cols = pl.ds(pl.multiple_of(g * HEAD_DIM, HEAD_DIM), HEAD_DIM)
        return [
            pltpu.make_async_copy(a.at[:, cols], b.at[:, cols], keep.at[i, g])
            for i, (a, b) in enumerate([(dk_buf, dk_hbm), (dv_buf, dv_hbm)])
        ]

    def tile(g, o):
        block = jnp.where(o == 0, me, last - me)
        start = doc_start(block)
        bias = [
            jnp.where(block - (REACH - kb) >= start, jnp.float32(0), jnp.float32(-jnp.inf))
            for kb in range(REACH + 1)
        ]
        q = head_rows(q_buf, o, g)
        do = head_rows(do_buf, o, g)
        keys = win[g, o, :, :HEAD_DIM]
        vals = win[g, o, :, HEAD_DIM:]
        s_ref[...] = dot_nt(keys, q)
        dp_ref[...] = dot_nt(vals, do)
        spans = [slice(kb * STRETCH, (kb + 1) * STRETCH) for kb in range(REACH + 1)]
        on_diag = jnp.where(later, -jnp.inf, s_ref[spans[REACH], :])
        s_ref[spans[REACH], :] = on_diag
        top = eights(on_diag, jnp.max)
        for kb in range(REACH):
            top = jnp.maximum(top, eights(s_ref[spans[kb], :], jnp.max) + bias[kb])
        top = jnp.max(top, axis=0, keepdims=True) * SCALE_LOG2E
        total = jnp.zeros((8, ROWS), jnp.float32)
        inner = jnp.zeros((8, ROWS), jnp.float32)
        for kb in range(REACH + 1):
            e = jnp.exp2(s_ref[spans[kb], :] * SCALE_LOG2E + (bias[kb] - top))
            s_ref[spans[kb], :] = e
            total = total + eights(e, jnp.sum)
            inner = inner + eights(e * dp_ref[spans[kb], :], jnp.sum)
        inverse = 1.0 / jnp.sum(total, axis=0, keepdims=True)
        inner = jnp.sum(inner, axis=0, keepdims=True) * inverse
        for kb in range(REACH + 1):
            p = s_ref[spans[kb], :] * inverse
            p_ref[spans[kb], :] = p.astype(jnp.bfloat16)
            ds_ref[spans[kb], :] = (p * (dp_ref[spans[kb], :] - inner)).astype(jnp.bfloat16)
        put_heads(o_buf, o, g, dot_nn(vals.T, p_ref[...]).astype(jnp.bfloat16).T)
        put_heads(dq_buf, o, g, (SCALE * dot_nn(keys.T, ds_ref[...])).astype(jnp.bfloat16).T)
        dv = dot_nn(p_ref[...], do)
        dk = SCALE * dot_nn(ds_ref[...], q)
        edge = REACH * STRETCH
        part[g, o, :edge, :HEAD_DIM] = dk[:edge].astype(jnp.bfloat16)
        part[g, o, :edge, HEAD_DIM:] = dv[:edge].astype(jnp.bfloat16)
        diag[g, o, :, :HEAD_DIM] = dk[edge:]
        diag[g, o, :, HEAD_DIM:] = dv[edge:]
        for copy in stores(g, o):
            copy.start()

    def send_home(g, device, slot):
        there, e = slot.source
        pltpu.make_async_remote_copy(
            part.at[g, slot.o, span(slot.k)], coming.at[g, e],
            rsend.at[g, slot.o, slot.k - 1], rrecv.at[g, e],
            device_id={"ctx": there}, device_id_type=MESH,
        ).start()

    def leaves(g, o):
        def emit(device):
            if o == 0:
                for low, high in twins(device):
                    twin = part[g, 1, span(high), :].astype(jnp.float32)
                    if low:
                        total = part[g, 0, span(low), :].astype(jnp.float32) + twin
                        part[g, 0, span(low), :] = total.astype(jnp.bfloat16)
                    else:
                        diag[g, 0] = diag[g, 0] + twin
            for slot in sorted(PLAN[device], key=lambda slot: -slot.level):
                if slot.k and slot.o == o and not slot.to:
                    send_home(g, device, slot)

        each_device(me, emit)

    def collect(level, g):
        def emit(device):
            for slot in PLAN[device]:
                if slot.level != level or not slot.to:
                    continue
                for _, e, _ in slot.to:
                    there = coming.at[g, e]
                    pltpu.make_async_copy(there, there, rrecv.at[g, e]).wait()
                if slot.k:
                    total = part[g, slot.o, span(slot.k), :].astype(jnp.float32)
                else:
                    total = diag[g, slot.o]
                for _, e, _ in slot.to:
                    total = total + coming[g, e].astype(jnp.float32)
                if slot.k:
                    part[g, slot.o, span(slot.k), :] = total.astype(jnp.bfloat16)
                    send_home(g, device, slot)
                else:
                    diag[g, slot.o] = total

        each_device(me, emit)
        if level == 0:
            cols = pl.ds(pl.multiple_of(g * HEAD_DIM, HEAD_DIM), HEAD_DIM)
            for o in range(2):
                rows = slice(o * STRETCH, (o + 1) * STRETCH)
                dk_buf[rows, cols] = diag[g, o, :, :HEAD_DIM].astype(jnp.bfloat16)
                dv_buf[rows, cols] = diag[g, o, :, HEAD_DIM:].astype(jnp.bfloat16)
            for copy in keeps(g):
                copy.start()

    tiles = 2 * KV_HEADS

    @pl.loop(-KV_HEADS, tiles + 2 * DEPTH)
    def _(turn):
        for level in range(DEPTH):
            g = turn + (KV_HEADS if level == 0 else DEPTH - level)

            @pl.when((g >= 0) & (g < KV_HEADS))
            def _():
                spread(level, g)

        @pl.when(turn == 0)
        def _():
            for copy in fetches[2:]:
                copy.wait()

        @pl.when((turn >= 0) & (turn < tiles))
        def _():
            g, second = turn // 2, lax.rem(turn, 2) == 0

            @pl.when(second)
            def _():
                complete(g)

            tile(g, jnp.where(second, 1, 0))

            @pl.when(second)
            def _():
                leaves(g, 1)

            @pl.when(jnp.logical_not(second))
            def _():
                leaves(g, 0)

        for level in range(DEPTH):
            since = turn - 1 - 2 * (DEPTH - level)

            @pl.when((since >= 0) & (lax.rem(since, 2) == 0) & (since < tiles))
            def _():
                collect(level, since // 2)

    @pl.loop(0, KV_HEADS)
    def _(g):
        def emit(device):
            for slot in PLAN[device]:
                for _, e, _ in slot.to:
                    here = win.at[g, 0, span(0)]
                    pltpu.make_async_copy(here, here, gsend.at[g, e]).wait()
                if slot.k:
                    here = part.at[g, slot.o, span(slot.k)]
                    pltpu.make_async_copy(here, here, rsend.at[g, slot.o, slot.k - 1]).wait()

        each_device(me, emit)
        for copy in stores(g, 0) + stores(g, 1) + keeps(g):
            copy.wait()


PIECES = 4


def hand_over(*refs):
    arrays, results, bufs, (arrive, leave) = refs[:4], refs[4:8], refs[8:12], refs[12:]
    inward, outward = [], []
    for i, (a, b, buf) in enumerate(zip(arrays, results, bufs, strict=True)):
        rows = a.shape[0] // PIECES
        for j in range(PIECES):
            piece = slice(j * rows, (j + 1) * rows)
            inward.append(pltpu.make_async_copy(a.at[piece], buf.at[piece], arrive.at[i, j]))
            outward.append(pltpu.make_async_copy(buf.at[piece], b.at[piece], leave.at[i, j]))
    for copy in inward:
        copy.start()
    for copy, after in zip(inward, outward, strict=True):
        copy.wait()
        after.start()
    for copy in outward:
        copy.wait()


def local(queries, keys, values, grad_out, doc_blocks):
    hbm = pl.BlockSpec(memory_space=pltpu.HBM)
    bf16, f32 = jnp.bfloat16, jnp.float32
    edge = pltpu.SemaphoreType.DMA((KV_HEADS, HOPS))
    slot = pltpu.SemaphoreType.DMA((KV_HEADS, 2, REACH))
    shapes = (
        jax.ShapeDtypeStruct(queries.shape, bf16),
        jax.ShapeDtypeStruct(queries.shape, bf16),
        jax.ShapeDtypeStruct(keys.shape, bf16),
        jax.ShapeDtypeStruct(values.shape, bf16),
    )
    results = pl.pallas_call(
        kernel,
        out_shape=shapes,
        in_specs=[hbm] * 5,
        out_specs=(hbm,) * 4,
        scratch_shapes=[
            pltpu.SMEM(doc_blocks.shape, jnp.int32),
            pltpu.VMEM(queries.shape, bf16),
            pltpu.VMEM(keys.shape, bf16),
            pltpu.VMEM(values.shape, bf16),
            pltpu.VMEM(queries.shape, bf16),
            pltpu.VMEM(queries.shape, bf16),
            pltpu.VMEM(queries.shape, bf16),
            pltpu.VMEM(keys.shape, bf16),
            pltpu.VMEM(values.shape, bf16),
            pltpu.VMEM((KV_HEADS, 2, WINDOW, PAIR), bf16),
            pltpu.VMEM((KV_HEADS, 2, REACH * STRETCH, PAIR), bf16),
            pltpu.VMEM((KV_HEADS, 2, STRETCH, PAIR), f32),
            pltpu.VMEM((KV_HEADS, HOPS, STRETCH, PAIR), bf16),
            pltpu.VMEM((WINDOW, ROWS), f32),
            pltpu.VMEM((WINDOW, ROWS), f32),
            pltpu.VMEM((WINDOW, ROWS), bf16),
            pltpu.VMEM((WINDOW, ROWS), bf16),
            pltpu.SemaphoreType.DMA((5,)),
            pltpu.SemaphoreType.DMA((2, KV_HEADS, 2)),
            pltpu.SemaphoreType.DMA((2, KV_HEADS)),
            edge, slot, slot, edge,
        ],
        compiler_params=pltpu.CompilerParams(
            collective_id=0, has_side_effects=True, vmem_limit_bytes=60 * 2**20
        ),
    )(doc_blocks, queries, keys, values, grad_out)
    return pl.pallas_call(
        hand_over,
        out_shape=shapes,
        in_specs=[hbm] * 4,
        out_specs=(hbm,) * 4,
        scratch_shapes=[pltpu.VMEM(a.shape, bf16) for a in shapes]
        + [pltpu.SemaphoreType.DMA((4, PIECES))] * 2,
        compiler_params=pltpu.CompilerParams(vmem_limit_bytes=60 * 2**20),
    )(*results)


def solution(mesh):
    token = P(("dp", "ctx"), None)
    return jax.shard_map(
        local, mesh=mesh, in_specs=(token, token, token, token, P("dp")),
        out_specs=(token,) * 4, check_vma=False,
    )
```

time: 88.5 us -> 60 us (0.68)
  the two profiles are of different devices: /device:TPU:218 before, /device:TPU:384 now
where the time goes in v2:
time: 60 us; the launch traced here: 59.9 us
  Pallas kernels  59.2 us (99%)
  between operations  0.64 us (1%)
    pallas_call x1, Pallas kernels, local(): pl.pallas_call(kernel, out_shape=shapes, in_specs=[hbm] * 5, out_specs=(h...  56.6 us
    pallas_call x1, Pallas kernels, local(): pl.pallas_call(hand_over, out_shape=shapes, in_specs=[hbm] * 4, out_specs...  2.61 us

profile of v2, /device:TPU:384, one launch (start us, length us, event | category | flops | bytes accessed | tf_op | source)
XLA Modules:
  0.0 59.9 jit_solution(11642553530815235737)
XLA Ops:
  0.6 56.6 %shard_map.84 = (bf16[128,4096]{1,0:T(8,128)(2,1)}, bf16[128,4096]{1,0:T(8,128)(2,1)}, bf16[128,512]{1,0:T(8,128)(2,1)}, bf16[128,512]{1,0:T(8,128)(2,1)}) custom-call(s32[8]{0:T(128)} %docs_hbm.1, bf16[128,4096]{1,0:T(8,128)(2,1)} %q_hbm.1, bf16[128,512]{1,0:T(8,128)(2,1)} %k_hbm.1, bf16[128,512]{1,0:T(8,128)(2,1)} %v_hbm.1, bf16[128,4096]{1,0:T(8,128)(2,1)} %do_hbm.1), custom_call_target="tpu_custom_call" | custom-call | tf_op jit(solution)/shard_map/pallas_call | solution.py:445
  57.2 2.6 %shard_map.85 = (bf16[128,4096]{1,0:T(8,128)(2,1)}, bf16[128,4096]{1,0:T(8,128)(2,1)}, bf16[128,512]{1,0:T(8,128)(2,1)}, bf16[128,512]{1,0:T(8,128)(2,1)}) custom-call(bf16[128,4096]{1,0:T(8,128)(2,1)} %get-tuple-element.8.refs_0_, bf16[128,4096]{1,0:T(8,128)(2,1)} %get-tuple-element.9.refs_1_, bf16[128,512]{1,0:T(8,128)(2,1)} %get-tuple-element.10.refs_2_, ...), custom_call_target="tpu_custom_call" | custom-call | tf_op jit(solution)/shard_map/pallas_call | solution.py:477

commit v3 on v2

--- a/solution.py
+++ b/solution.py
@@ -27,42 +27,78 @@
     return lax.dot_general(a, b, (((1,), (0,)), ((), ())), preferred_element_type=jnp.float32)
 
 
-N, LAST, DEPTH = 16, 31, 3
-
-TREE = (
-    (0, 0, 0, 0, 1, 2, 6, 0,),
-    (3, 1, 5, 1, 2, 3, 4, 1,),
-    (2, 6, 6, 2, 4, 10, 5, 2,),
-    (7, 4, 7, 3, 4, 11, 6, 7,),
-    (4, 5, 4, 4, 5, 6, 8, 4,),
-    (7, 5, 9, 5, 6, 8, 8, 5,),
-    (6, 10, 8, 6, 7, 8, 14, 10,),
-    (12, 11, 14, 7, 15, 9, 15, 7,),
-    (8, 9, 8, 8, 12, 10, 11,),
+N, LAST = 16, 31
+
+DOWN = (
+    (0, 1, 7, 0, 1, 2, 4, 4,),
+    (1, 2, 5, 1, 5, 3, 9, 5,),
+    (2, 7, 6, 2, 3, 4, 5, 9,),
+    (5, 6, 7, 3, 11, 5, 6, 7,),
+    (4, 10, 4, 4, 8, 9, 8, 8,),
+    (10, 11, 9, 5, 9, 10, 8, 9,),
+    (6, 9, 10, 6, 7, 13, 9, 10,),
+    (11, 8, 11, 7, 8, 14, 10, 12,),
+    (8, 14, 8, 8, 12, 13, 14,),
     (9, 10, 13, 9, 13, 12,),
-    (10, 13, 14, 10, 14,),
-    (15, 14, 15, 11,),
-    (15, 12, 12, 12,),
-    (14, 15, 13, 13, 14,),
-    (13, 14, 15, 13, 14, 14,),
-    (12, 13, 11, 15, 15, 12, 15,),
-    (15, 12, 13, 9, 7, 15, 15, 13,),
-    (10, 11, 11, 10, 14, 10, 14, 9,),
-    (9, 5, 11, 9, 13, 11, 9, 8,),
-    (8, 9, 10, 11, 12, 8, 8, 8,),
-    (7, 7, 6, 7, 11, 4, 10, 11,),
-    (6, 7, 8, 6, 10, 6, 10, 5,),
-    (9, 6, 1, 8, 9, 5, 3, 9,),
-    (8, 0, 6, 7, 8, 1, 4, 4,),
-    (3, 5, 3, 7, 7, 4, 2,),
-    (4, 2, 6, 2, 5, 6,),
-    (3, 5, 1, 1, 5,),
-    (4, 0, 1, 0,),
+    (10, 15, 12, 10, 11,),
+    (15, 12, 15, 11,),
+    (15, 12, 15, 12,),
+    (14, 15, 13, 13, 12,),
+    (10, 14, 15, 15, 9, 14,),
+    (11, 8, 14, 15, 13, 14, 15,),
+    (11, 12, 8, 11, 15, 15, 12, 10,),
+    (10, 11, 12, 13, 14, 10, 13, 14,),
+    (9, 5, 6, 9, 13, 9, 8, 8,),
+    (8, 4, 5, 4, 12, 5, 11, 8,),
+    (7, 8, 6, 7, 11, 11, 8, 6,),
+    (6, 7, 7, 9, 10, 6, 4, 10,),
+    (5, 6, 2, 5, 9, 5, 6, 9,),
+    (1, 5, 1, 7, 8, 4, 7, 4,),
+    (4, 0, 3, 7, 7, 1, 2,),
+    (3, 2, 6, 2, 0, 6,),
+    (1, 5, 3, 0, 5,),
+    (4, 0, 3, 0,),
     (3, 2, 3,),
     (1, 2,),
     (1,),
     (),
 )
+UP = (
+    (2, 3, 0, 0, 4, 2, 3, 4,),
+    (1, 2, 5, 1, 5, 4, 9, 5,),
+    (2, 7, 6, 2, 3, 4, 10, 6,),
+    (7, 6, 7, 3, 4, 5, 11, 7,),
+    (4, 5, 6, 4, 5, 11, 8, 8,),
+    (5, 6, 9, 5, 6, 8, 13, 9,),
+    (11, 9, 10, 6, 10, 13, 14, 10,),
+    (11, 8, 11, 7, 8, 12, 10, 11,),
+    (8, 9, 10, 8, 12, 13, 14,),
+    (9, 15, 13, 9, 15, 12,),
+    (10, 15, 14, 10, 11,),
+    (15, 12, 15, 11,),
+    (15, 14, 15, 12,),
+    (14, 15, 13, 13, 14,),
+    (13, 9, 15, 13, 14, 14,),
+    (12, 13, 14, 8, 15, 14, 15,),
+    (11, 11, 8, 11, 15, 15, 12, 13,),
+    (10, 6, 12, 8, 14, 10, 13, 14,),
+    (6, 10, 6, 12, 13, 9, 10, 13,),
+    (7, 9, 7, 11, 12, 8, 9, 8,),
+    (7, 7, 4, 7, 11, 9, 10, 11,),
+    (6, 7, 8, 4, 10, 6, 9, 10,),
+    (5, 1, 7, 8, 9, 7, 4, 9,),
+    (4, 5, 1, 0, 8, 4, 7, 4,),
+    (3, 2, 6, 2, 5, 6, 7,),
+    (3, 0, 6, 2, 0, 6,),
+    (1, 5, 1, 2, 5,),
+    (4, 2, 3, 0,),
+    (3, 0, 3,),
+    (1, 2,),
+    (1,),
+    (),
+)
+DOWN_TURNS = (8, 5, 3, 1)
+UP_TURNS = (17, 12, 6, 2)
 
 
 def holder(block):
@@ -82,34 +118,37 @@
         self.level, self.to, self.source = level, [], None
 
 
-def build():
+def build(tree):
     plan = [[] for _ in range(N)]
     count = [0] * N
-    for block, parents in enumerate(TREE):
+    for block, parents in enumerate(tree):
         top = min(block + REACH, LAST)
         readers = sorted({holder(b) for b in range(block + 1, top + 1)} - {holder(block)})
-        slots = {holder(block): Slot(holder(block), block, 0)}
-        left = dict(zip(readers, parents, strict=True))
-        while left:
-            for device, source in sorted(left.items()):
-                if source in slots and device not in slots and slots[source].level < DEPTH:
-                    slots[device] = Slot(device, block, slots[source].level + 1)
-                    slots[device].source = (source, count[source])
-                    slots[source].to.append((device, count[source], slots[device]))
-                    count[source] += 1
-                    del left[device]
-        for device, slot in slots.items():
+        source = dict(zip(readers, parents, strict=True))
+        level = {holder(block): 0}
+        while len(level) <= len(readers):
+            for device in readers:
+                if device not in level and source[device] in level:
+                    level[device] = level[source[device]] + 1
+        slots = {}
+        for device in sorted(level, key=lambda device: (level[device], device)):
+            slots[device] = slot = Slot(device, block, level[device])
             plan[device].append(slot)
+            if slot.level:
+                near = source[device]
+                slot.source = (near, count[near])
+                slots[near].to.append((device, count[near], slot))
+                count[near] += 1
     return plan, max(count)
 
 
-PLAN, HOPS = build()
+(DOWN_PLAN, DOWN_HOPS), (UP_PLAN, UP_HOPS) = build(DOWN), build(UP)
 NEAR = [
     sorted(
-        {hop[0] for slot in slots for hop in slot.to}
-        | {slot.source[0] for slot in slots if slot.source}
+        {hop[0] for slot in down + up for hop in slot.to}
+        | {slot.source[0] for slot in down + up if slot.source}
     )
-    for slots in PLAN
+    for down, up in zip(DOWN_PLAN, UP_PLAN, strict=True)
 ]
 
 
@@ -174,7 +213,7 @@
 
     def spread(level, g):
         def emit(device):
-            for slot in PLAN[device]:
+            for slot in DOWN_PLAN[device]:
                 if slot.level != level or not slot.to:
                     continue
                 if slot.k:
@@ -194,7 +233,7 @@
 
     def complete(g):
         def emit(device):
-            for slot in PLAN[device]:
+            for slot in DOWN_PLAN[device]:
                 if slot.k and not slot.to:
                     arrived(g, slot)
             for low, high in twins(device):
@@ -317,7 +356,7 @@
                         part[g, 0, span(low), :] = total.astype(jnp.bfloat16)
                     else:
                         diag[g, 0] = diag[g, 0] + twin
-            for slot in sorted(PLAN[device], key=lambda slot: -slot.level):
+            for slot in sorted(UP_PLAN[device], key=lambda slot: -slot.level):
                 if slot.k and slot.o == o and not slot.to:
                     send_home(g, device, slot)
 
@@ -325,7 +364,7 @@
 
     def collect(level, g):
         def emit(device):
-            for slot in PLAN[device]:
+            for slot in UP_PLAN[device]:
                 if slot.level != level or not slot.to:
                     continue
                 for _, e, _ in slot.to:
@@ -355,10 +394,10 @@
 
     tiles = 2 * KV_HEADS
 
-    @pl.loop(-KV_HEADS, tiles + 2 * DEPTH)
+    @pl.loop(-max(DOWN_TURNS), tiles + max(UP_TURNS))
     def _(turn):
-        for level in range(DEPTH):
-            g = turn + (KV_HEADS if level == 0 else DEPTH - level)
+        for level, ahead in enumerate(DOWN_TURNS):
+            g = turn + ahead
 
             @pl.when((g >= 0) & (g < KV_HEADS))
             def _():
@@ -387,8 +426,8 @@
             def _():
                 leaves(g, 0)
 
-        for level in range(DEPTH):
-            since = turn - 1 - 2 * (DEPTH - level)
+        for level, behind in enumerate(UP_TURNS):
+            since = turn - 1 - behind
 
             @pl.when((since >= 0) & (lax.rem(since, 2) == 0) & (since < tiles))
             def _():
@@ -397,10 +436,11 @@
     @pl.loop(0, KV_HEADS)
     def _(g):
         def emit(device):
-            for slot in PLAN[device]:
+            for slot in DOWN_PLAN[device]:
                 for _, e, _ in slot.to:
                     here = win.at[g, 0, span(0)]
                     pltpu.make_async_copy(here, here, gsend.at[g, e]).wait()
+            for slot in UP_PLAN[device]:
                 if slot.k:
                     here = part.at[g, slot.o, span(slot.k)]
                     pltpu.make_async_copy(here, here, rsend.at[g, slot.o, slot.k - 1]).wait()
@@ -434,7 +474,8 @@
 def local(queries, keys, values, grad_out, doc_blocks):
     hbm = pl.BlockSpec(memory_space=pltpu.HBM)
     bf16, f32 = jnp.bfloat16, jnp.float32
-    edge = pltpu.SemaphoreType.DMA((KV_HEADS, HOPS))
+    down = pltpu.SemaphoreType.DMA((KV_HEADS, DOWN_HOPS))
+    up = pltpu.SemaphoreType.DMA((KV_HEADS, UP_HOPS))
     slot = pltpu.SemaphoreType.DMA((KV_HEADS, 2, REACH))
     shapes = (
         jax.ShapeDtypeStruct(queries.shape, bf16),
@@ -460,7 +501,7 @@
             pltpu.VMEM((KV_HEADS, 2, WINDOW, PAIR), bf16),
             pltpu.VMEM((KV_HEADS, 2, REACH * STRETCH, PAIR), bf16),
             pltpu.VMEM((KV_HEADS, 2, STRETCH, PAIR), f32),
-            pltpu.VMEM((KV_HEADS, HOPS, STRETCH, PAIR), bf16),
+            pltpu.VMEM((KV_HEADS, UP_HOPS, STRETCH, PAIR), bf16),
             pltpu.VMEM((WINDOW, ROWS), f32),
             pltpu.VMEM((WINDOW, ROWS), f32),
             pltpu.VMEM((WINDOW, ROWS), bf16),
@@ -468,7 +509,7 @@
             pltpu.SemaphoreType.DMA((5,)),
             pltpu.SemaphoreType.DMA((2, KV_HEADS, 2)),
             pltpu.SemaphoreType.DMA((2, KV_HEADS)),
-            edge, slot, slot, edge,
+            down, slot, slot, up,
         ],
         compiler_params=pltpu.CompilerParams(
             collective_id=0, has_side_effects=True, vmem_limit_bytes=60 * 2**20

time: 60 us -> 56.2 us (0.937)
  the two profiles are of different devices: /device:TPU:384 before, /device:TPU:16 now
where the time goes in v3:
time: 56.2 us; the launch traced here: 56 us
  Pallas kernels  55.4 us (99%)
  between operations  0.64 us (1%)
    pallas_call x1, Pallas kernels, local(): pl.pallas_call(kernel, out_shape=shapes, in_specs=[hbm] * 5, out_specs=(h...  52.8 us
    pallas_call x1, Pallas kernels, local(): pl.pallas_call(hand_over, out_shape=shapes, in_specs=[hbm] * 4, out_specs...  2.61 us

profile of v3, /device:TPU:16, one launch (start us, length us, event | category | flops | bytes accessed | tf_op | source)
XLA Modules:
  0.0 56.0 jit_solution(5186628267398649798)
XLA Ops:
  0.6 52.8 %shard_map.84 = (bf16[128,4096]{1,0:T(8,128)(2,1)}, bf16[128,4096]{1,0:T(8,128)(2,1)}, bf16[128,512]{1,0:T(8,128)(2,1)}, bf16[128,512]{1,0:T(8,128)(2,1)}) custom-call(s32[8]{0:T(128)} %docs_hbm.1, bf16[128,4096]{1,0:T(8,128)(2,1)} %q_hbm.1, bf16[128,512]{1,0:T(8,128)(2,1)} %k_hbm.1, bf16[128,512]{1,0:T(8,128)(2,1)} %v_hbm.1, bf16[128,4096]{1,0:T(8,128)(2,1)} %do_hbm.1), custom_call_target="tpu_custom_call" | custom-call | tf_op jit(solution)/shard_map/pallas_call | solution.py:486
  53.4 2.6 %shard_map.85 = (bf16[128,4096]{1,0:T(8,128)(2,1)}, bf16[128,4096]{1,0:T(8,128)(2,1)}, bf16[128,512]{1,0:T(8,128)(2,1)}, bf16[128,512]{1,0:T(8,128)(2,1)}) custom-call(bf16[128,4096]{1,0:T(8,128)(2,1)} %get-tuple-element.8.refs_0_, bf16[128,4096]{1,0:T(8,128)(2,1)} %get-tuple-element.9.refs_1_, bf16[128,512]{1,0:T(8,128)(2,1)} %get-tuple-element.10.refs_2_, ...), custom_call_target="tpu_custom_call" | custom-call | tf_op jit(solution)/shard_map/pallas_call | solution.py:518

commit v4 on v3

--- a/solution.py
+++ b/solution.py
@@ -30,33 +30,33 @@
 N, LAST = 16, 31
 
 DOWN = (
-    (0, 1, 7, 0, 1, 2, 4, 4,),
-    (1, 2, 5, 1, 5, 3, 9, 5,),
-    (2, 7, 6, 2, 3, 4, 5, 9,),
-    (5, 6, 7, 3, 11, 5, 6, 7,),
-    (4, 10, 4, 4, 8, 9, 8, 8,),
-    (10, 11, 9, 5, 9, 10, 8, 9,),
-    (6, 9, 10, 6, 7, 13, 9, 10,),
-    (11, 8, 11, 7, 8, 14, 10, 12,),
-    (8, 14, 8, 8, 12, 13, 14,),
-    (9, 10, 13, 9, 13, 12,),
-    (10, 15, 12, 10, 11,),
+    (0, 3, 0, 0, 1, 7, 3, 4,),
+    (1, 2, 5, 1, 5, 3, 4, 5,),
+    (2, 5, 6, 2, 4, 4, 5, 6,),
+    (7, 4, 5, 3, 4, 5, 11, 7,),
+    (4, 5, 4, 4, 8, 9, 7, 8,),
+    (5, 6, 9, 5, 6, 8, 13, 9,),
+    (6, 11, 13, 6, 10, 13, 14, 10,),
+    (11, 10, 11, 7, 8, 9, 10, 14,),
+    (8, 9, 15, 8, 9, 15, 12,),
+    (9, 15, 13, 9, 15, 12,),
+    (10, 15, 14, 10, 11,),
     (15, 12, 15, 11,),
     (15, 12, 15, 12,),
-    (14, 15, 13, 13, 12,),
-    (10, 14, 15, 15, 9, 14,),
-    (11, 8, 14, 15, 13, 14, 15,),
-    (11, 12, 8, 11, 15, 15, 12, 10,),
-    (10, 11, 12, 13, 14, 10, 13, 14,),
-    (9, 5, 6, 9, 13, 9, 8, 8,),
-    (8, 4, 5, 4, 12, 5, 11, 8,),
-    (7, 8, 6, 7, 11, 11, 8, 6,),
-    (6, 7, 7, 9, 10, 6, 4, 10,),
-    (5, 6, 2, 5, 9, 5, 6, 9,),
-    (1, 5, 1, 7, 8, 4, 7, 4,),
-    (4, 0, 3, 7, 7, 1, 2,),
+    (14, 15, 15, 13, 14,),
+    (10, 14, 10, 15, 14, 14,),
+    (11, 13, 11, 15, 15, 12, 10,),
+    (11, 12, 13, 14, 15, 15, 12, 15,),
+    (10, 6, 12, 10, 14, 10, 13, 14,),
+    (9, 5, 6, 9, 13, 9, 10, 13,),
+    (8, 9, 7, 11, 12, 8, 9, 8,),
+    (7, 7, 6, 7, 11, 11, 8, 6,),
+    (6, 2, 8, 6, 10, 6, 9, 10,),
+    (5, 1, 2, 8, 9, 2, 4, 9,),
+    (4, 0, 3, 7, 8, 1, 7, 4,),
+    (3, 0, 3, 7, 7, 4, 2,),
     (3, 2, 6, 2, 0, 6,),
-    (1, 5, 3, 0, 5,),
+    (4, 5, 1, 0, 5,),
     (4, 0, 3, 0,),
     (3, 2, 3,),
     (1, 2,),
@@ -64,41 +64,41 @@
     (),
 )
 UP = (
-    (2, 3, 0, 0, 4, 2, 3, 4,),
-    (1, 2, 5, 1, 5, 4, 9, 5,),
-    (2, 7, 6, 2, 3, 4, 10, 6,),
-    (7, 6, 7, 3, 4, 5, 11, 7,),
-    (4, 5, 6, 4, 5, 11, 8, 8,),
-    (5, 6, 9, 5, 6, 8, 13, 9,),
-    (11, 9, 10, 6, 10, 13, 14, 10,),
-    (11, 8, 11, 7, 8, 12, 10, 11,),
-    (8, 9, 10, 8, 12, 13, 14,),
-    (9, 15, 13, 9, 15, 12,),
-    (10, 15, 14, 10, 11,),
+    (2, 0, 2, 0, 4, 5, 4, 4,),
+    (3, 1, 5, 1, 2, 4, 4, 5,),
+    (2, 5, 6, 2, 3, 10, 5, 2,),
+    (7, 7, 7, 3, 11, 8, 11, 3,),
+    (4, 7, 4, 4, 5, 6, 8, 8,),
+    (7, 5, 9, 5, 6, 7, 13, 5,),
+    (6, 11, 10, 6, 7, 13, 14, 6,),
+    (12, 11, 14, 7, 15, 9, 15, 7,),
+    (13, 11, 8, 8, 12, 13, 12,),
+    (9, 10, 13, 9, 12, 11,),
+    (10, 13, 14, 10, 14,),
     (15, 12, 15, 11,),
-    (15, 14, 15, 12,),
-    (14, 15, 13, 13, 14,),
-    (13, 9, 15, 13, 14, 14,),
-    (12, 13, 14, 8, 15, 14, 15,),
-    (11, 11, 8, 11, 15, 15, 12, 13,),
-    (10, 6, 12, 8, 14, 10, 13, 14,),
-    (6, 10, 6, 12, 13, 9, 10, 13,),
-    (7, 9, 7, 11, 12, 8, 9, 8,),
-    (7, 7, 4, 7, 11, 9, 10, 11,),
-    (6, 7, 8, 4, 10, 6, 9, 10,),
-    (5, 1, 7, 8, 9, 7, 4, 9,),
-    (4, 5, 1, 0, 8, 4, 7, 4,),
-    (3, 2, 6, 2, 5, 6, 7,),
-    (3, 0, 6, 2, 0, 6,),
-    (1, 5, 1, 2, 5,),
-    (4, 2, 3, 0,),
-    (3, 0, 3,),
+    (15, 12, 15, 12,),
+    (14, 15, 15, 13, 14,),
+    (13, 14, 10, 13, 14, 14,),
+    (12, 13, 14, 15, 15, 12, 15,),
+    (15, 12, 8, 14, 15, 15, 14, 12,),
+    (10, 11, 9, 10, 14, 10, 14, 9,),
+    (13, 5, 6, 9, 13, 6, 8, 8,),
+    (12, 9, 10, 4, 12, 8, 8, 8,),
+    (11, 7, 4, 10, 11, 11, 8, 11,),
+    (6, 2, 8, 9, 10, 6, 9, 10,),
+    (5, 1, 1, 8, 9, 5, 4, 9,),
+    (4, 0, 0, 7, 8, 4, 7, 4,),
+    (4, 5, 3, 7, 5, 7, 2,),
+    (2, 2, 6, 2, 5, 6,),
+    (1, 5, 1, 0, 0,),
+    (4, 0, 0, 0,),
+    (1, 2, 3,),
     (1, 2,),
     (1,),
     (),
 )
-DOWN_TURNS = (8, 5, 3, 1)
-UP_TURNS = (17, 12, 6, 2)
+DOWN_TURNS = (8, 5, 3, 2)
+UP_TURNS = (16, 10, 4)
 
 
 def holder(block):
@@ -293,49 +293,65 @@
             for i, (a, b) in enumerate([(dk_buf, dk_hbm), (dv_buf, dv_hbm)])
         ]
 
-    def tile(g, o):
-        block = jnp.where(o == 0, me, last - me)
+    spans = [slice(kb * STRETCH, (kb + 1) * STRETCH) for kb in range(REACH + 1)]
+
+    def products(g, o):
+        q = head_rows(q_buf, o, g)
+        do = head_rows(do_buf, o, g)
+        s_ref[o] = dot_nt(win[g, o, :, :HEAD_DIM], q)
+        dp_ref[o] = dot_nt(win[g, o, :, HEAD_DIM:], do)
+
+    def weights(o):
+        block = last - me if o else me
         start = doc_start(block)
         bias = [
             jnp.where(block - (REACH - kb) >= start, jnp.float32(0), jnp.float32(-jnp.inf))
             for kb in range(REACH + 1)
         ]
-        q = head_rows(q_buf, o, g)
-        do = head_rows(do_buf, o, g)
-        keys = win[g, o, :, :HEAD_DIM]
-        vals = win[g, o, :, HEAD_DIM:]
-        s_ref[...] = dot_nt(keys, q)
-        dp_ref[...] = dot_nt(vals, do)
-        spans = [slice(kb * STRETCH, (kb + 1) * STRETCH) for kb in range(REACH + 1)]
-        on_diag = jnp.where(later, -jnp.inf, s_ref[spans[REACH], :])
-        s_ref[spans[REACH], :] = on_diag
+        on_diag = jnp.where(later, -jnp.inf, s_ref[o, spans[REACH], :])
+        s_ref[o, spans[REACH], :] = on_diag
         top = eights(on_diag, jnp.max)
         for kb in range(REACH):
-            top = jnp.maximum(top, eights(s_ref[spans[kb], :], jnp.max) + bias[kb])
+            top = jnp.maximum(top, eights(s_ref[o, spans[kb], :], jnp.max) + bias[kb])
         top = jnp.max(top, axis=0, keepdims=True) * SCALE_LOG2E
         total = jnp.zeros((8, ROWS), jnp.float32)
         inner = jnp.zeros((8, ROWS), jnp.float32)
         for kb in range(REACH + 1):
-            e = jnp.exp2(s_ref[spans[kb], :] * SCALE_LOG2E + (bias[kb] - top))
-            s_ref[spans[kb], :] = e
+            e = jnp.exp2(s_ref[o, spans[kb], :] * SCALE_LOG2E + (bias[kb] - top))
+            s_ref[o, spans[kb], :] = e
             total = total + eights(e, jnp.sum)
-            inner = inner + eights(e * dp_ref[spans[kb], :], jnp.sum)
+            inner = inner + eights(e * dp_ref[o, spans[kb], :], jnp.sum)
         inverse = 1.0 / jnp.sum(total, axis=0, keepdims=True)
         inner = jnp.sum(inner, axis=0, keepdims=True) * inverse
         for kb in range(REACH + 1):
-            p = s_ref[spans[kb], :] * inverse
-            p_ref[spans[kb], :] = p.astype(jnp.bfloat16)
-            ds_ref[spans[kb], :] = (p * (dp_ref[spans[kb], :] - inner)).astype(jnp.bfloat16)
-        put_heads(o_buf, o, g, dot_nn(vals.T, p_ref[...]).astype(jnp.bfloat16).T)
-        put_heads(dq_buf, o, g, (SCALE * dot_nn(keys.T, ds_ref[...])).astype(jnp.bfloat16).T)
-        dv = dot_nn(p_ref[...], do)
-        dk = SCALE * dot_nn(ds_ref[...], q)
+            p = s_ref[o, spans[kb], :] * inverse
+            p_ref[o, spans[kb], :] = p.astype(jnp.bfloat16)
+            ds = p * (dp_ref[o, spans[kb], :] - inner)
+            ds_ref[o, spans[kb], :] = ds.astype(jnp.bfloat16)
+
+    def gradients(g, o):
+        dv = dot_nn(p_ref[o], head_rows(do_buf, o, g))
+        dk = SCALE * dot_nn(ds_ref[o], head_rows(q_buf, o, g))
         edge = REACH * STRETCH
         part[g, o, :edge, :HEAD_DIM] = dk[:edge].astype(jnp.bfloat16)
         part[g, o, :edge, HEAD_DIM:] = dv[:edge].astype(jnp.bfloat16)
         diag[g, o, :, :HEAD_DIM] = dk[edge:]
         diag[g, o, :, HEAD_DIM:] = dv[edge:]
-        for copy in stores(g, o):
+
+    def outputs(g, o):
+        vals = win[g, o, :, HEAD_DIM:]
+        keys = win[g, o, :, :HEAD_DIM]
+        put_heads(o_buf, o, g, dot_nn(vals.T, p_ref[o]).astype(jnp.bfloat16).T)
+        put_heads(dq_buf, o, g, (SCALE * dot_nn(keys.T, ds_ref[o])).astype(jnp.bfloat16).T)
+
+    def pair(g):
+        for o in (1, 0):
+            products(g, o)
+        for o in (1, 0):
+            weights(o)
+            gradients(g, o)
+            outputs(g, o)
+        for copy in stores(g, 1) + stores(g, 0):
             copy.start()
 
     def send_home(g, device, slot):
@@ -408,23 +424,13 @@
             for copy in fetches[2:]:
                 copy.wait()
 
-        @pl.when((turn >= 0) & (turn < tiles))
+        @pl.when((turn >= 0) & (turn < tiles) & (lax.rem(turn, 2) == 0))
         def _():
-            g, second = turn // 2, lax.rem(turn, 2) == 0
-
-            @pl.when(second)
-            def _():
-                complete(g)
-
-            tile(g, jnp.where(second, 1, 0))
-
-            @pl.when(second)
-            def _():
-                leaves(g, 1)
-
-            @pl.when(jnp.logical_not(second))
-            def _():
-                leaves(g, 0)
+            g = turn // 2
+            complete(g)
+            pair(g)
+            leaves(g, 1)
+            leaves(g, 0)
 
         for level, behind in enumerate(UP_TURNS):
             since = turn - 1 - behind
@@ -502,10 +508,10 @@
             pltpu.VMEM((KV_HEADS, 2, REACH * STRETCH, PAIR), bf16),
             pltpu.VMEM((KV_HEADS, 2, STRETCH, PAIR), f32),
             pltpu.VMEM((KV_HEADS, UP_HOPS, STRETCH, PAIR), bf16),
-            pltpu.VMEM((WINDOW, ROWS), f32),
-            pltpu.VMEM((WINDOW, ROWS), f32),
-            pltpu.VMEM((WINDOW, ROWS), bf16),
-            pltpu.VMEM((WINDOW, ROWS), bf16),
+            pltpu.VMEM((2, WINDOW, ROWS), f32),
+            pltpu.VMEM((2, WINDOW, ROWS), f32),
+            pltpu.VMEM((2, WINDOW, ROWS), bf16),
+            pltpu.VMEM((2, WINDOW, ROWS), bf16),
             pltpu.SemaphoreType.DMA((5,)),
             pltpu.SemaphoreType.DMA((2, KV_HEADS, 2)),
             pltpu.SemaphoreType.DMA((2, KV_HEADS)),

time: 56.2 us -> 53 us (0.943)
  the two profiles are of different devices: /device:TPU:16 before, /device:TPU:472 now
where the time goes in v4:
time: 53 us; the launch traced here: 52.8 us
  Pallas kernels  52.2 us (98%)
  between operations  0.64 us (1%)
    pallas_call x1, Pallas kernels, local(): pl.pallas_call(kernel, out_shape=shapes, in_specs=[hbm] * 5, out_specs=(h...  49.6 us
    pallas_call x1, Pallas kernels, local(): pl.pallas_call(hand_over, out_shape=shapes, in_specs=[hbm] * 4, out_specs...  2.61 us

profile of v4, /device:TPU:472, one launch (start us, length us, event | category | flops | bytes accessed | tf_op | source)
XLA Modules:
  0.0 52.8 jit_solution(10725453095743631368)
XLA Ops:
  0.6 49.6 %shard_map.84 = (bf16[128,4096]{1,0:T(8,128)(2,1)}, bf16[128,4096]{1,0:T(8,128)(2,1)}, bf16[128,512]{1,0:T(8,128)(2,1)}, bf16[128,512]{1,0:T(8,128)(2,1)}) custom-call(s32[8]{0:T(128)} %docs_hbm.1, bf16[128,4096]{1,0:T(8,128)(2,1)} %q_hbm.1, bf16[128,512]{1,0:T(8,128)(2,1)} %k_hbm.1, bf16[128,512]{1,0:T(8,128)(2,1)} %v_hbm.1, bf16[128,4096]{1,0:T(8,128)(2,1)} %do_hbm.1), custom_call_target="tpu_custom_call" | custom-call | tf_op jit(solution)/shard_map/pallas_call | solution.py:492
  50.2 2.6 %shard_map.85 = (bf16[128,4096]{1,0:T(8,128)(2,1)}, bf16[128,4096]{1,0:T(8,128)(2,1)}, bf16[128,512]{1,0:T(8,128)(2,1)}, bf16[128,512]{1,0:T(8,128)(2,1)}) custom-call(bf16[128,4096]{1,0:T(8,128)(2,1)} %get-tuple-element.8.refs_0_, bf16[128,4096]{1,0:T(8,128)(2,1)} %get-tuple-element.9.refs_1_, bf16[128,512]{1,0:T(8,128)(2,1)} %get-tuple-element.10.refs_2_, ...), custom_call_target="tpu_custom_call" | custom-call | tf_op jit(solution)/shard_map/pallas_call | solution.py:524

commit v5 on v4

--- a/solution.py
+++ b/solution.py
@@ -153,11 +153,21 @@
 
 
 def each_device(me, emit):
-    for device in range(N):
-
-        @pl.when(me == device)
+    def halve(low, high):
+        if high - low == 1:
+            emit(low)
+            return
+        middle = (low + high) // 2
+
+        @pl.when(me < middle)
         def _():
-            emit(device)
+            halve(low, middle)
+
+        @pl.when(me >= middle)
+        def _():
+            halve(middle, high)
+
+    halve(0, N)
 
 
 def span(k):
@@ -172,6 +182,13 @@
     me = lax.axis_index("ctx")
     last = LAST
 
+    barrier = pltpu.get_barrier_semaphore()
+
+    def greet(device):
+        for near in NEAR[device]:
+            pl.semaphore_signal(barrier, inc=1, device_id={"ctx": near}, device_id_type=MESH)
+
+    each_device(me, greet)
     fetches = [
         pltpu.make_async_copy(a, b, fetch.at[i])
         for i, (a, b) in enumerate(
@@ -181,13 +198,6 @@
     for copy in fetches:
         copy.start()
 
-    barrier = pltpu.get_barrier_semaphore()
-
-    def greet(device):
-        for near in NEAR[device]:
-            pl.semaphore_signal(barrier, inc=1, device_id={"ctx": near}, device_id_type=MESH)
-
-    each_device(me, greet)
     fetches[0].wait()
     fetches[1].wait()
     for g in range(KV_HEADS):

time: 53 us -> 49.4 us (0.932)
  the two profiles are of different devices: /device:TPU:472 before, /device:TPU:222 now
where the time goes in v5:
time: 49.4 us; the launch traced here: 49.2 us
  Pallas kernels  48.6 us (98%)
  between operations  0.64 us (1%)
    pallas_call x1, Pallas kernels, local(): pl.pallas_call(kernel, out_shape=shapes, in_specs=[hbm] * 5, out_specs=(h...  46 us
    pallas_call x1, Pallas kernels, local(): pl.pallas_call(hand_over, out_shape=shapes, in_specs=[hbm] * 4, out_specs...  2.61 us

profile of v5, /device:TPU:222, one launch (start us, length us, event | category | flops | bytes accessed | tf_op | source)
XLA Modules:
  0.0 49.2 jit_solution(5651046576373154280)
XLA Ops:
  0.6 46.0 %shard_map.84 = (bf16[128,4096]{1,0:T(8,128)(2,1)}, bf16[128,4096]{1,0:T(8,128)(2,1)}, bf16[128,512]{1,0:T(8,128)(2,1)}, bf16[128,512]{1,0:T(8,128)(2,1)}) custom-call(s32[8]{0:T(128)} %docs_hbm.1, bf16[128,4096]{1,0:T(8,128)(2,1)} %q_hbm.1, bf16[128,512]{1,0:T(8,128)(2,1)} %k_hbm.1, bf16[128,512]{1,0:T(8,128)(2,1)} %v_hbm.1, bf16[128,4096]{1,0:T(8,128)(2,1)} %do_hbm.1), custom_call_target="tpu_custom_call" | custom-call | tf_op jit(solution)/shard_map/pallas_call | solution.py:502
  46.6 2.6 %shard_map.85 = (bf16[128,4096]{1,0:T(8,128)(2,1)}, bf16[128,4096]{1,0:T(8,128)(2,1)}, bf16[128,512]{1,0:T(8,128)(2,1)}, bf16[128,512]{1,0:T(8,128)(2,1)}) custom-call(bf16[128,4096]{1,0:T(8,128)(2,1)} %get-tuple-element.8.refs_0_, bf16[128,4096]{1,0:T(8,128)(2,1)} %get-tuple-element.9.refs_1_, bf16[128,512]{1,0:T(8,128)(2,1)} %get-tuple-element.10.refs_2_, ...), custom_call_target="tpu_custom_call" | custom-call | tf_op jit(solution)/shard_map/pallas_call | solution.py:534
